TPU v7x, 32 devices: a whole 2x2x4 slice. The times are simulated.
32 devices in a mesh: groups: 2 (over y), trades: 8 (over z, x), dates: 2 (over core).
Axes of the slice: x: 2, y: 2, z: 4, core: 2. Of those that a mesh axis runs over, the one named last changes fastest.
Arguments:
- basis_values: bfloat16 [8, 256, 256], P('dates', 'groups'), parts along dimension 1, may hold values from -6 to 6
- coefficients: bfloat16 [8192, 256], P('trades'), may hold values from -0.0625 to 0.0625
- set_map: int32 [8192], P('trades'), may hold values from 0 to 255, as said below
- trade_type: int32 [8192], P('trades'), may hold values from 0 to 15
- type_gain: float32 [8, 16], P('dates'), may hold values from 0.25 to 4
- set_lags: int32 [256], replicated, may hold values from 1 to 2
- thresholds: float32 [256], replicated, may hold values from -1 to 1
Outputs:
- coef_grad: float32 [16384, 256], P(('groups', 'trades'), 'dates'), parts along dimension 0
There are 2 independent parts, one for each index of `groups`. A program takes and returns all parts, laid end to end along the dimension named above; an argument that names none is the same for every part. Nothing has to cross between parts.
Inputs may be any that keep to these rules, and one draw needn't show every extreme that they name: `set_map`: in every aligned block of 1024 trades, exactly 128 trades fall in each group of 32 consecutive netting sets (sets g * 32 to (g + 1) * 32 - 1).
All inputs are finite; a program needn't handle non-finite values.
Results may differ from a plain program's by a relative error of at most 0.0018.
Values may be sent and summed in bfloat16 or wider, within the bound.
A program may use at most 64 MiB of HBM per device.

v0:
```python
import functools
import math

import jax
import jax.numpy as jnp
from jax import lax
from jax.experimental import pallas as pl
from jax.experimental.pallas import tpu as pltpu
from jax.sharding import PartitionSpec as P

LAG_MAX = 2
GROUP = 8
PIECES = 2
CODE_MAX = 32767.0
NT = (((1,), (1,)), ((), ()))


def kernel(
    trade_peers, date_peers, loss_scale,
    gain_in, basis_in, coef_in, set_in, type_in, lag_in, limit_in,
    out_ref,
    gain_ref, basis_ref, coef_ref, set_ref, type_ref, lag_ref, limit_ref, load_sem,
    code_send, code_recv, unit_send, unit_recv, adj_send, adj_recv,
    member_ref, gain_cols, basis_rows, scaled_ref, half_send, half_recv,
    code_ss, code_rs, unit_ss, unit_rs, adj_ss, adj_rs, half_ss, half_rs,
):
    peers = trade_peers * date_peers
    my_trade = lax.axis_index("trades")
    my_date = lax.axis_index("dates")
    me = my_trade * date_peers + my_date
    local_dates, path_count, basis_count = basis_ref.shape
    trade_count = coef_ref.shape[0]
    set_count = limit_ref.shape[1]
    type_count = gain_ref.shape[1]
    own_paths = path_count // peers
    groups = peers // GROUP
    group_paths = GROUP * own_paths
    group_rows = local_dates * group_paths
    chunk_rows = local_dates * own_paths
    half = basis_count // date_peers

    def device(index):
        return {"trades": index // date_peers, "dates": index % date_peers}

    barrier = pltpu.get_barrier_semaphore()

    def greet(step, carry):
        pl.semaphore_signal(
            barrier, inc=1, device_id=device(lax.rem(me + step, peers)),
            device_id_type=pl.DeviceIdType.MESH,
        )
        return carry

    lax.fori_loop(1, peers, greet, 0, unroll=peers <= 16)
    loads = [
        pltpu.make_async_copy(source, target, load_sem.at[i])
        for i, (source, target) in enumerate((
            (type_in, type_ref), (gain_in, gain_ref), (set_in, set_ref), (basis_in, basis_ref),
            (coef_in, coef_ref), (lag_in, lag_ref), (limit_in, limit_ref),
        ))
    ]
    for load in loads:
        load.start()
    for load in loads[:3]:
        load.wait()

    def code_copy(index, slot_here, slot_there):
        return pltpu.make_async_remote_copy(
            src_ref=code_send.at[slot_here], dst_ref=code_recv.at[slot_there],
            send_sem=code_ss.at[slot_here], recv_sem=code_rs.at[slot_there],
            device_id=device(index), device_id_type=pl.DeviceIdType.MESH,
        )

    def unit_copy(index, slot_here, slot_there):
        return pltpu.make_async_remote_copy(
            src_ref=unit_send.at[slot_here], dst_ref=unit_recv.at[slot_there],
            send_sem=unit_ss.at[slot_here], recv_sem=unit_rs.at[slot_there],
            device_id=device(index), device_id_type=pl.DeviceIdType.MESH,
        )

    def adj_copy(index, slot_there):
        return pltpu.make_async_remote_copy(
            src_ref=adj_send.at[index % date_peers], dst_ref=adj_recv.at[slot_there],
            send_sem=adj_ss.at[index], recv_sem=adj_rs.at[slot_there],
            device_id=device(index), device_id_type=pl.DeviceIdType.MESH,
        )

    types = type_ref[...]
    table = gain_ref[...]
    gains = []
    for d in range(local_dates):
        row = jnp.zeros_like(types, dtype=jnp.float32)
        for y in range(type_count):
            row = jnp.where(types == y, table[d:d + 1, y:y + 1], row)
        gains.append(row)
    set_ids = lax.broadcasted_iota(jnp.int32, (set_count, trade_count), 0)
    member_wide = jnp.where(set_ids == set_ref[...], 1.0, 0.0)
    member = member_wide.astype(jnp.bfloat16)

    my_group = me // GROUP
    for load in loads[3:]:
        load.wait()

    def forward(step, carry):
        group = lax.rem(my_group + 1 + step, groups)
        rows = basis_ref[:, pl.ds(pl.multiple_of(group * group_paths, group_paths), group_paths), :]
        raw = lax.dot_general(
            rows.reshape(group_rows, basis_count), coef_ref[...], NT,
            preferred_element_type=jnp.float32,
        )
        prices = jnp.concatenate(
            [raw[d * group_paths:(d + 1) * group_paths] * gains[d] for d in range(local_dates)], axis=0
        ).astype(jnp.bfloat16)
        part = lax.dot_general(prices, member, NT, preferred_element_type=jnp.float32)
        part = part.reshape(local_dates, GROUP, own_paths, set_count)
        for i in range(GROUP):
            chunk = part[:, i].reshape(chunk_rows, set_count)
            top = jnp.maximum(jnp.max(jnp.abs(chunk), axis=0, keepdims=True), 1e-30)
            codes = jnp.round(chunk * (CODE_MAX / top)).astype(jnp.int32)
            code_send[group * GROUP + i] = codes.astype(jnp.int16)
            unit_send[group * GROUP + i] = top * (1.0 / CODE_MAX)

        return carry

    lax.fori_loop(0, groups, forward, 0, unroll=groups <= 2)
    pl.semaphore_wait(barrier, peers - 1)

    def deal(step, carry):
        index = lax.rem(me + step, peers)
        code_copy(index, index, me).start()
        unit_copy(index, index, me).start()
        return carry

    lax.fori_loop(1, peers, deal, 0, unroll=peers <= 16)

    code_recv[me] = code_send[me]
    unit_recv[me] = unit_send[me]
    member_ref[...] = jnp.transpose(member_wide).astype(jnp.bfloat16)
    gain_rows = jnp.concatenate(
        [jnp.broadcast_to(gains[d], (group_paths, trade_count)) for d in range(local_dates)], axis=0
    )
    gain_cols[...] = jnp.transpose(gain_rows)

    def order_rows(group, carry):
        rows = basis_ref[:, pl.ds(pl.multiple_of(group * group_paths, group_paths), group_paths), :]
        basis_rows[pl.ds(pl.multiple_of(group * group_rows, group_rows), group_rows), :] = (
            rows.reshape(group_rows, basis_count)
        )
        return carry

    lax.fori_loop(0, groups, order_rows, 0, unroll=groups <= 2)

    def arrived(step, carry):
        source = lax.rem(me + step, peers)
        code_copy(source, source, source).wait_recv()
        unit_copy(source, source, source).wait_recv()
        return carry

    lax.fori_loop(1, peers, arrived, 0, unroll=peers <= 16)

    def add(trade, totals):
        result = []
        for q in range(date_peers):
            source = trade * date_peers + q
            values = code_recv[source].astype(jnp.int32).astype(jnp.float32)
            result.append(totals[q] + values * unit_recv[source])
        return tuple(result)

    totals = lax.fori_loop(
        0, trade_peers, add,
        tuple(jnp.zeros((chunk_rows, set_count), jnp.float32) for _ in range(date_peers)),
        unroll=peers <= 16,
    )
    netted = [
        totals[q][d * own_paths:(d + 1) * own_paths]
        for q in range(date_peers) for d in range(local_dates)
    ]
    date_count = len(netted)
    lags = lag_ref[...]
    direct = []
    for d in range(date_count):
        value = netted[d]
        for lag in range(1, LAG_MAX + 1):
            if d >= lag:
                value = value - jnp.where(lags == lag, netted[d - lag], 0.0)
        direct.append(jnp.maximum(value - limit_ref[...], 0.0) * loss_scale)
    for q in range(date_peers):
        parts = []
        for d in range(q * local_dates, (q + 1) * local_dates):
            value = direct[d]
            for lag in range(1, LAG_MAX + 1):
                if d + lag < date_count:
                    value = value - jnp.where(lags == lag, direct[d + lag], 0.0)
            parts.append(value)
        adj_send[q] = jnp.concatenate(parts, axis=0).astype(jnp.bfloat16)

    def spread_out(step, carry):
        adj_copy(lax.rem(me + step, peers), me).start()
        return carry

    lax.fori_loop(1, peers, spread_out, 0, unroll=peers <= 16)
    adj_recv[me] = adj_send[my_date]

    def backward(step, carry):
        group = lax.rem(my_group + step, groups)
        for i in range(GROUP):
            index = group * GROUP + i

            @pl.when(index != me)
            def _():
                adj_copy(index, index).wait_recv()

        block = adj_recv[pl.ds(pl.multiple_of(group * GROUP, GROUP), GROUP)].astype(jnp.float32)
        block = block.reshape(GROUP, local_dates, own_paths, set_count)
        block = jnp.concatenate(
            [block[i, d] for d in range(local_dates) for i in range(GROUP)], axis=0
        ).astype(jnp.bfloat16)
        spread = lax.dot_general(member_ref[...], block, NT, preferred_element_type=jnp.float32)
        scaled_ref[:, pl.ds(pl.multiple_of(group * group_rows, group_rows), group_rows)] = (
            spread * gain_cols[...]
        ).astype(jnp.bfloat16)
        return carry

    lax.fori_loop(0, groups, backward, 0, unroll=groups <= 2)

    piece_rows = trade_count // PIECES

    def half_copy(step, piece):
        rows = pl.ds(piece * piece_rows, piece_rows)
        q = lax.rem(my_date + step, date_peers)
        return pltpu.make_async_remote_copy(
            src_ref=half_send.at[step - 1, rows], dst_ref=half_recv.at[step - 1, rows],
            send_sem=half_ss.at[step - 1, piece], recv_sem=half_rs.at[step - 1, piece],
            device_id={"dates": q}, device_id_type=pl.DeviceIdType.MESH,
        )

    def columns(q):
        return basis_rows[:, pl.ds(pl.multiple_of(q * half, half), half)]

    for step in range(1, date_peers):
        q = lax.rem(my_date + step, date_peers)
        for piece in range(PIECES):
            rows = pl.ds(piece * piece_rows, piece_rows)
            half_send[step - 1, rows] = jnp.dot(
                scaled_ref[rows], columns(q), preferred_element_type=jnp.float32
            )
            half_copy(step, piece).start()
    out_ref[...] = jnp.dot(scaled_ref[...], columns(my_date), preferred_element_type=jnp.float32)

    def sent(step, carry):
        index = lax.rem(me + step, peers)
        code_copy(index, index, me).wait_send()
        unit_copy(index, index, me).wait_send()
        adj_copy(index, me).wait_send()
        return carry

    lax.fori_loop(1, peers, sent, 0, unroll=peers <= 16)
    for step in range(1, date_peers):
        for piece in range(PIECES):
            rows = pl.ds(piece * piece_rows, piece_rows)
            half_copy(step, piece).wait_recv()
            out_ref[rows] += half_recv[step - 1, rows]

    for step in range(1, date_peers):
        for piece in range(PIECES):
            half_copy(step, piece).wait_send()


def on_device(
    trade_peers, date_peers,
    basis_values, coefficients, set_map, trade_type, type_gain, set_lags, thresholds,
):
    local_dates, path_count, basis_count = basis_values.shape
    trade_count = coefficients.shape[0]
    set_count = thresholds.shape[0]
    peers = trade_peers * date_peers
    own_paths = path_count // peers
    chunk = local_dates * own_paths
    group_rows = chunk * GROUP
    half = basis_count // date_peers
    loss_scale = 2.0 / math.sqrt(local_dates * date_peers * path_count)
    vmem_limit = min(60, 20 + 4 * local_dates * path_count // 512) * 1024 * 1024
    vmem = pl.BlockSpec(memory_space=pltpu.VMEM)
    dma = pltpu.SemaphoreType.DMA
    return pl.pallas_call(
        functools.partial(kernel, trade_peers, date_peers, loss_scale),
        out_shape=jax.ShapeDtypeStruct((trade_count, half), jnp.float32),
        in_specs=[pl.BlockSpec(memory_space=pltpu.HBM)] * 7,
        out_specs=vmem,
        scratch_shapes=[
            pltpu.VMEM(type_gain.shape, jnp.float32),
            pltpu.VMEM(basis_values.shape, jnp.bfloat16),
            pltpu.VMEM(coefficients.shape, jnp.bfloat16),
            pltpu.VMEM((1, trade_count), jnp.int32),
            pltpu.VMEM((1, trade_count), jnp.int32),
            pltpu.VMEM((1, set_count), jnp.int32),
            pltpu.VMEM((1, set_count), jnp.float32),
            dma((7,)),
            pltpu.VMEM((peers, chunk, set_count), jnp.int16),
            pltpu.VMEM((peers, chunk, set_count), jnp.int16),
            pltpu.VMEM((peers, 1, set_count), jnp.float32),
            pltpu.VMEM((peers, 1, set_count), jnp.float32),
            pltpu.VMEM((date_peers, chunk, set_count), jnp.bfloat16),
            pltpu.VMEM((peers, chunk, set_count), jnp.bfloat16),
            pltpu.VMEM((trade_count, set_count), jnp.bfloat16),
            pltpu.VMEM((trade_count, group_rows), jnp.float32),
            pltpu.VMEM((path_count * local_dates, basis_count), jnp.bfloat16),
            pltpu.VMEM((trade_count, path_count * local_dates), jnp.bfloat16),
            pltpu.VMEM((date_peers - 1, trade_count, half), jnp.float32),
            pltpu.VMEM((date_peers - 1, trade_count, half), jnp.float32),
            dma((peers,)), dma((peers,)), dma((peers,)), dma((peers,)),
            dma((peers,)), dma((peers,)), dma((date_peers - 1, PIECES)), dma((date_peers - 1, PIECES)),
        ],
        compiler_params=pltpu.CompilerParams(
            collective_id=0, has_side_effects=True, vmem_limit_bytes=vmem_limit
        ),
    )(
        *[
            pltpu.with_memory_space_constraint(x, pltpu.HBM)
            for x in (
                type_gain, basis_values, coefficients, set_map.reshape(1, -1),
                trade_type.reshape(1, -1), set_lags.reshape(1, -1), thresholds.reshape(1, -1),
            )
        ]
    )


def solution(mesh):
    return jax.shard_map(
        functools.partial(on_device, mesh.shape["trades"], mesh.shape["dates"]),
        mesh=mesh,
        in_specs=(
            P("dates", "groups", None),
            P("trades", None),
            P("trades"),
            P("trades"),
            P("dates", None),
            P(),
            P(),
        ),
        out_specs=P(("groups", "trades"), "dates"),
        check_vma=False,
    )
```

profile of v0, /device:TPU:17, one launch (start us, length us, event | category | flops | bytes accessed | tf_op | source)
XLA Modules:
  0.0 23.0 jit_solution(7018437515823641670)
XLA Ops:
  0.0 22.2 %shard_map.73 = f32[1024,128]{1,0:T(8,128)S(1)} custom-call(f32[4,16]{1,0:T(4,128)} %gain_in.1, bf16[4,128,256]{2,1,0:T(8,128)(2,1)} %basis_in.1, bf16[1024,256]{1,0:T(8,128)(2,1)} %coef_in.1, s32[1,1024]{1,0:T(1,128)} %bitcast.4, s32[1,1024]{1,0:T(1,128)} %bitcast.5, s32[1,256]{1,0:T(1,128)} %bitcast.6, f32[1,256]{1,0:T(1,128)} %bitcast.7), custom_call_target="tpu_custom_call" | custom-call | tf_op jit(solution)/shard_map/pallas_call | solution.py:285
  22.2 0.8 %copy.9 = f32[1024,128]{1,0:T(8,128)} copy(f32[1024,128]{1,0:T(8,128)S(1)} %shard_map.73) | data formatting | bytes 1048576
where the time goes:
time: 23.1 us; the launch traced here: 23 us
  Pallas kernels  22.2 us (96%)
  local copies, waits for them, and re-layouts  0.8 us (3%)
    pallas_call x1, Pallas kernels, on_device(): pl.pallas_call(functools.partial(kernel, trade_peers, date_peers, loss_sc...  22.2 us
    unnamed x1, local copies, waits for them, and re-layouts  0.8 us

commit v1 on v0

--- a/solution.py
+++ b/solution.py
@@ -10,7 +10,7 @@
 
 LAG_MAX = 2
 GROUP = 8
-PIECES = 2
+PIECES = 4
 CODE_MAX = 32767.0
 NT = (((1,), (1,)), ((), ()))
 
@@ -21,26 +21,37 @@
     out_ref,
     gain_ref, basis_ref, coef_ref, set_ref, type_ref, lag_ref, limit_ref, load_sem,
     code_send, code_recv, unit_send, unit_recv, adj_send, adj_recv,
-    member_ref, gain_cols, basis_rows, scaled_ref, half_send, half_recv,
+    member_ref, gain_cols, basis_rows, total_ref, half_recv,
     code_ss, code_rs, unit_ss, unit_rs, adj_ss, adj_rs, half_ss, half_rs,
 ):
     peers = trade_peers * date_peers
     my_trade = lax.axis_index("trades")
     my_date = lax.axis_index("dates")
-    me = my_trade * date_peers + my_date
+    me = my_date * trade_peers + my_trade
     local_dates, path_count, basis_count = basis_ref.shape
     trade_count = coef_ref.shape[0]
     set_count = limit_ref.shape[1]
     type_count = gain_ref.shape[1]
     own_paths = path_count // peers
     groups = peers // GROUP
+    wave_groups = trade_peers // GROUP
     group_paths = GROUP * own_paths
     group_rows = local_dates * group_paths
     chunk_rows = local_dates * own_paths
     half = basis_count // date_peers
+    unroll = peers <= 16
 
     def device(index):
-        return {"trades": index // date_peers, "dates": index % date_peers}
+        return {"trades": index % trade_peers, "dates": index // trade_peers}
+
+    def partner(step):
+        trade = 0
+        for bit in range((trade_peers - 1).bit_length()):
+            weight = 2 ** bit
+            mine = (my_trade // weight) % 2
+            flip = (step // weight) % 2
+            trade += weight * (mine + flip - 2 * mine * flip)
+        return trade
 
     barrier = pltpu.get_barrier_semaphore()
 
@@ -51,7 +62,7 @@
         )
         return carry
 
-    lax.fori_loop(1, peers, greet, 0, unroll=peers <= 16)
+    lax.fori_loop(1, peers, greet, 0, unroll=unroll)
     loads = [
         pltpu.make_async_copy(source, target, load_sem.at[i])
         for i, (source, target) in enumerate((
@@ -80,7 +91,7 @@
 
     def adj_copy(index, slot_there):
         return pltpu.make_async_remote_copy(
-            src_ref=adj_send.at[index % date_peers], dst_ref=adj_recv.at[slot_there],
+            src_ref=adj_send.at[index // trade_peers], dst_ref=adj_recv.at[slot_there],
             send_sem=adj_ss.at[index], recv_sem=adj_rs.at[slot_there],
             device_id=device(index), device_id_type=pl.DeviceIdType.MESH,
         )
@@ -97,12 +108,10 @@
     member_wide = jnp.where(set_ids == set_ref[...], 1.0, 0.0)
     member = member_wide.astype(jnp.bfloat16)
 
-    my_group = me // GROUP
     for load in loads[3:]:
         load.wait()
 
-    def forward(step, carry):
-        group = lax.rem(my_group + 1 + step, groups)
+    def forward(group, carry):
         rows = basis_ref[:, pl.ds(pl.multiple_of(group * group_paths, group_paths), group_paths), :]
         raw = lax.dot_general(
             rows.reshape(group_rows, basis_count), coef_ref[...], NT,
@@ -122,16 +131,26 @@
 
         return carry
 
-    lax.fori_loop(0, groups, forward, 0, unroll=groups <= 2)
-    pl.semaphore_wait(barrier, peers - 1)
-
-    def deal(step, carry):
-        index = lax.rem(me + step, peers)
-        code_copy(index, index, me).start()
-        unit_copy(index, index, me).start()
-        return carry
-
-    lax.fori_loop(1, peers, deal, 0, unroll=peers <= 16)
+    for wave in range(date_peers):
+        lax.fori_loop(
+            wave * wave_groups, (wave + 1) * wave_groups, forward, 0, unroll=wave_groups <= 1
+        )
+        if wave == 0:
+            pl.semaphore_wait(barrier, peers - 1)
+
+        def deal(step, carry):
+            index = wave * trade_peers + partner(trade_peers - step)
+            code_copy(index, index, me).start()
+            unit_copy(index, index, me).start()
+            return carry
+
+        lax.fori_loop(1, trade_peers, deal, 0, unroll=unroll)
+
+        @pl.when(my_date != wave)
+        def _():
+            index = wave * trade_peers + my_trade
+            code_copy(index, index, me).start()
+            unit_copy(index, index, me).start()
 
     code_recv[me] = code_send[me]
     unit_recv[me] = unit_send[me]
@@ -140,6 +159,8 @@
         [jnp.broadcast_to(gains[d], (group_paths, trade_count)) for d in range(local_dates)], axis=0
     )
     gain_cols[...] = jnp.transpose(gain_rows)
+    if groups > 2:
+        total_ref[...] = jnp.zeros_like(total_ref)
 
     def order_rows(group, carry):
         rows = basis_ref[:, pl.ds(pl.multiple_of(group * group_paths, group_paths), group_paths), :]
@@ -156,12 +177,12 @@
         unit_copy(source, source, source).wait_recv()
         return carry
 
-    lax.fori_loop(1, peers, arrived, 0, unroll=peers <= 16)
+    lax.fori_loop(1, peers, arrived, 0, unroll=unroll)
 
     def add(trade, totals):
         result = []
         for q in range(date_peers):
-            source = trade * date_peers + q
+            source = q * trade_peers + trade
             values = code_recv[source].astype(jnp.int32).astype(jnp.float32)
             result.append(totals[q] + values * unit_recv[source])
         return tuple(result)
@@ -169,7 +190,7 @@
     totals = lax.fori_loop(
         0, trade_peers, add,
         tuple(jnp.zeros((chunk_rows, set_count), jnp.float32) for _ in range(date_peers)),
-        unroll=peers <= 16,
+        unroll=unroll,
     )
     netted = [
         totals[q][d * own_paths:(d + 1) * own_paths]
@@ -195,14 +216,17 @@
         adj_send[q] = jnp.concatenate(parts, axis=0).astype(jnp.bfloat16)
 
     def spread_out(step, carry):
-        adj_copy(lax.rem(me + step, peers), me).start()
-        return carry
-
-    lax.fori_loop(1, peers, spread_out, 0, unroll=peers <= 16)
+        trade = partner(trade_peers - step)
+        for q in range(date_peers):
+            adj_copy(q * trade_peers + trade, me).start()
+        return carry
+
+    lax.fori_loop(1, trade_peers, spread_out, 0, unroll=unroll)
+    for step in range(1, date_peers):
+        adj_copy(lax.rem(my_date + step, date_peers) * trade_peers + my_trade, me).start()
     adj_recv[me] = adj_send[my_date]
 
-    def backward(step, carry):
-        group = lax.rem(my_group + step, groups)
+    def block_of(group):
         for i in range(GROUP):
             index = group * GROUP + i
 
@@ -212,40 +236,50 @@
 
         block = adj_recv[pl.ds(pl.multiple_of(group * GROUP, GROUP), GROUP)].astype(jnp.float32)
         block = block.reshape(GROUP, local_dates, own_paths, set_count)
-        block = jnp.concatenate(
+        return jnp.concatenate(
             [block[i, d] for d in range(local_dates) for i in range(GROUP)], axis=0
         ).astype(jnp.bfloat16)
-        spread = lax.dot_general(member_ref[...], block, NT, preferred_element_type=jnp.float32)
-        scaled_ref[:, pl.ds(pl.multiple_of(group * group_rows, group_rows), group_rows)] = (
-            spread * gain_cols[...]
-        ).astype(jnp.bfloat16)
-        return carry
-
-    lax.fori_loop(0, groups, backward, 0, unroll=groups <= 2)
 
     piece_rows = trade_count // PIECES
+
+    def gradient(group, block, first, count):
+        rows = pl.ds(first, count)
+        spread = lax.dot_general(member_ref[rows], block, NT, preferred_element_type=jnp.float32)
+        scaled = (spread * gain_cols[rows]).astype(jnp.bfloat16)
+        return jnp.dot(
+            scaled, basis_rows[pl.ds(pl.multiple_of(group * group_rows, group_rows), group_rows), :],
+            preferred_element_type=jnp.float32,
+        )
+
+    def keep(rows, part, fresh):
+        for q in range(date_peers):
+            columns = part[:, q * half:(q + 1) * half]
+            total_ref[q, rows] = columns if fresh else total_ref[q, rows] + columns
+
+    def backward(group, carry):
+        block = block_of(group)
+        for piece in range(PIECES):
+            part = gradient(group, block, piece * piece_rows, piece_rows)
+            keep(pl.ds(piece * piece_rows, piece_rows), part, groups <= 2)
+        return carry
+
+    lax.fori_loop(0, groups - 1, backward, 0, unroll=groups <= 2)
 
     def half_copy(step, piece):
         rows = pl.ds(piece * piece_rows, piece_rows)
         q = lax.rem(my_date + step, date_peers)
         return pltpu.make_async_remote_copy(
-            src_ref=half_send.at[step - 1, rows], dst_ref=half_recv.at[step - 1, rows],
+            src_ref=total_ref.at[q, rows], dst_ref=half_recv.at[step - 1, rows],
             send_sem=half_ss.at[step - 1, piece], recv_sem=half_rs.at[step - 1, piece],
             device_id={"dates": q}, device_id_type=pl.DeviceIdType.MESH,
         )
 
-    def columns(q):
-        return basis_rows[:, pl.ds(pl.multiple_of(q * half, half), half)]
-
-    for step in range(1, date_peers):
-        q = lax.rem(my_date + step, date_peers)
-        for piece in range(PIECES):
-            rows = pl.ds(piece * piece_rows, piece_rows)
-            half_send[step - 1, rows] = jnp.dot(
-                scaled_ref[rows], columns(q), preferred_element_type=jnp.float32
-            )
+    last = block_of(groups - 1)
+    for piece in range(PIECES):
+        part = gradient(groups - 1, last, piece * piece_rows, piece_rows)
+        keep(pl.ds(piece * piece_rows, piece_rows), part, groups == 1)
+        for step in range(1, date_peers):
             half_copy(step, piece).start()
-    out_ref[...] = jnp.dot(scaled_ref[...], columns(my_date), preferred_element_type=jnp.float32)
 
     def sent(step, carry):
         index = lax.rem(me + step, peers)
@@ -254,12 +288,14 @@
         adj_copy(index, me).wait_send()
         return carry
 
-    lax.fori_loop(1, peers, sent, 0, unroll=peers <= 16)
-    for step in range(1, date_peers):
-        for piece in range(PIECES):
-            rows = pl.ds(piece * piece_rows, piece_rows)
+    lax.fori_loop(1, peers, sent, 0, unroll=unroll)
+    for piece in range(PIECES):
+        rows = pl.ds(piece * piece_rows, piece_rows)
+        result = total_ref[my_date, rows]
+        for step in range(1, date_peers):
             half_copy(step, piece).wait_recv()
-            out_ref[rows] += half_recv[step - 1, rows]
+            result += half_recv[step - 1, rows]
+        out_ref[rows] = result
 
     for step in range(1, date_peers):
         for piece in range(PIECES):
@@ -305,8 +341,7 @@
             pltpu.VMEM((trade_count, set_count), jnp.bfloat16),
             pltpu.VMEM((trade_count, group_rows), jnp.float32),
             pltpu.VMEM((path_count * local_dates, basis_count), jnp.bfloat16),
-            pltpu.VMEM((trade_count, path_count * local_dates), jnp.bfloat16),
-            pltpu.VMEM((date_peers - 1, trade_count, half), jnp.float32),
+            pltpu.VMEM((date_peers, trade_count, half), jnp.float32),
             pltpu.VMEM((date_peers - 1, trade_count, half), jnp.float32),
             dma((peers,)), dma((peers,)), dma((peers,)), dma((peers,)),
             dma((peers,)), dma((peers,)), dma((date_peers - 1, PIECES)), dma((date_peers - 1, PIECES)),

time: 23.1 us -> 23.9 us (1.035)
  the two profiles are of different devices: /device:TPU:17 before, /device:TPU:1 now
where the time goes in v1:
time: 23.9 us; the launch traced here: 23.6 us
  Pallas kernels  22.8 us (95%)
  local copies, waits for them, and re-layouts  0.8 us (3%)
    pallas_call x1, Pallas kernels, on_device(): pl.pallas_call(functools.partial(kernel, trade_peers, date_peers, loss_sc...  22.8 us
    unnamed x1, local copies, waits for them, and re-layouts  0.8 us

profile of v1, /device:TPU:1, one launch (start us, length us, event | category | flops | bytes accessed | tf_op | source)
XLA Modules:
  0.0 23.6 jit_solution(8905748717622261595)
XLA Ops:
  0.0 22.8 %shard_map.73 = f32[1024,128]{1,0:T(8,128)S(1)} custom-call(f32[4,16]{1,0:T(4,128)} %gain_in.1, bf16[4,128,256]{2,1,0:T(8,128)(2,1)} %basis_in.1, bf16[1024,256]{1,0:T(8,128)(2,1)} %coef_in.1, s32[1,1024]{1,0:T(1,128)} %bitcast.4, s32[1,1024]{1,0:T(1,128)} %bitcast.5, s32[1,256]{1,0:T(1,128)} %bitcast.6, f32[1,256]{1,0:T(1,128)} %bitcast.7), custom_call_target="tpu_custom_call" | custom-call | tf_op jit(solution)/shard_map/pallas_call | solution.py:321
  22.8 0.8 %copy.9 = f32[1024,128]{1,0:T(8,128)} copy(f32[1024,128]{1,0:T(8,128)S(1)} %shard_map.73) | data formatting | bytes 1048576

commit v2 on v1

v2 whole, which is shorter than its diff:
```python
import functools
import math

import jax
import jax.numpy as jnp
from jax import lax
from jax.experimental import pallas as pl
from jax.experimental.pallas import tpu as pltpu
from jax.sharding import PartitionSpec as P

LAG_MAX = 2
GROUP = 8
PIECES = 2
WAVES = 2
CODE_MAX = 32767.0
NT = (((1,), (1,)), ((), ()))


def kernel(
    trade_peers, loss_scale,
    gain_in, basis_in, coef_in, set_in, type_in, lag_in, limit_in,
    out_ref,
    gain_ref, basis_ref, coef_ref, set_ref, type_ref, lag_ref, limit_ref, load_sem,
    code_send, code_recv, unit_send, unit_recv, edge_send, edge_recv, adj_send, adj_recv,
    member_ref, gain_cols, basis_rows, total_ref, half_recv,
    code_ss, code_rs, unit_ss, unit_rs, edge_ss, edge_rs, adj_ss, adj_rs, half_ss, half_rs,
):
    my_trade = lax.axis_index("trades")
    my_date = lax.axis_index("dates")
    local_dates, path_count, basis_count = basis_ref.shape
    trade_count = coef_ref.shape[0]
    set_count = limit_ref.shape[1]
    type_count = gain_ref.shape[1]
    others = trade_peers - 1
    own_paths = path_count // (WAVES * trade_peers)
    wave_groups = trade_peers // GROUP
    groups = WAVES * wave_groups
    group_paths = GROUP * own_paths
    group_rows = local_dates * group_paths
    chunk_rows = local_dates * own_paths
    edge_rows = LAG_MAX * own_paths
    half = basis_count // 2
    unroll = trade_peers <= 8

    def partner(step):
        trade = 0
        for bit in range(others.bit_length()):
            weight = 2 ** bit
            mine = (my_trade // weight) % 2
            flip = (step // weight) % 2
            trade += weight * (mine + flip - 2 * mine * flip)
        return trade

    barrier = pltpu.get_barrier_semaphore()

    def greet(step, carry):
        pl.semaphore_signal(
            barrier, inc=1, device_id={"trades": partner(trade_peers - step)},
            device_id_type=pl.DeviceIdType.MESH,
        )
        return carry

    lax.fori_loop(1, trade_peers, greet, 0, unroll=unroll)
    pl.semaphore_signal(
        barrier, inc=1, device_id={"dates": 1 - my_date}, device_id_type=pl.DeviceIdType.MESH
    )
    loads = [
        pltpu.make_async_copy(source, target, load_sem.at[i])
        for i, (source, target) in enumerate((
            (type_in, type_ref), (gain_in, gain_ref), (set_in, set_ref), (basis_in, basis_ref),
            (coef_in, coef_ref), (lag_in, lag_ref), (limit_in, limit_ref),
        ))
    ]
    for load in loads:
        load.start()
    for load in loads[:3]:
        load.wait()

    def to_trade(source, target, send_sem, recv_sem, trade):
        return pltpu.make_async_remote_copy(
            src_ref=source, dst_ref=target, send_sem=send_sem, recv_sem=recv_sem,
            device_id={"trades": trade}, device_id_type=pl.DeviceIdType.MESH,
        )

    def to_core(source, target, send_sem, recv_sem):
        return pltpu.make_async_remote_copy(
            src_ref=source, dst_ref=target, send_sem=send_sem, recv_sem=recv_sem,
            device_id={"dates": 1 - my_date}, device_id_type=pl.DeviceIdType.MESH,
        )

    def code_copy(wave, here, there, trade):
        return to_trade(code_send.at[here], code_recv.at[there], code_ss.at[0], code_rs.at[wave], trade)

    def unit_copy(wave, here, there, trade):
        return to_trade(unit_send.at[here], unit_recv.at[there], unit_ss.at[0], unit_rs.at[wave], trade)

    def adj_copy(wave, here, there, trade):
        return to_trade(adj_send.at[here], adj_recv.at[there], adj_ss.at[0], adj_rs.at[wave], trade)

    def all_of(buffer, send_sem, recv_sem, count):
        slots = buffer.at[pl.ds(0, count)]
        return to_trade(slots, slots, send_sem, recv_sem, my_trade)

    types = type_ref[...]
    table = gain_ref[...]
    gains = []
    for d in range(local_dates):
        row = jnp.zeros_like(types, dtype=jnp.float32)
        for y in range(type_count):
            row = jnp.where(types == y, table[d:d + 1, y:y + 1], row)
        gains.append(row)
    set_ids = lax.broadcasted_iota(jnp.int32, (set_count, trade_count), 0)
    member_wide = jnp.where(set_ids == set_ref[...], 1.0, 0.0)
    member = member_wide.astype(jnp.bfloat16)

    for load in loads[3:]:
        load.wait()

    def forward(group, carry):
        rows = basis_ref[:, pl.ds(pl.multiple_of(group * group_paths, group_paths), group_paths), :]
        raw = lax.dot_general(
            rows.reshape(group_rows, basis_count), coef_ref[...], NT,
            preferred_element_type=jnp.float32,
        )
        prices = jnp.concatenate(
            [raw[d * group_paths:(d + 1) * group_paths] * gains[d] for d in range(local_dates)], axis=0
        ).astype(jnp.bfloat16)
        part = lax.dot_general(prices, member, NT, preferred_element_type=jnp.float32)
        part = part.reshape(local_dates, GROUP, own_paths, set_count)
        for i in range(GROUP):
            chunk = part[:, i].reshape(chunk_rows, set_count)
            top = jnp.maximum(jnp.max(jnp.abs(chunk), axis=0, keepdims=True), 1e-30)
            codes = jnp.round(chunk * (CODE_MAX / top)).astype(jnp.int32)
            code_send[group * GROUP + i] = codes.astype(jnp.int16)
            unit_send[group * GROUP + i] = top * (1.0 / CODE_MAX)

        return carry

    for wave in range(WAVES):
        lax.fori_loop(
            wave * wave_groups, (wave + 1) * wave_groups, forward, 0, unroll=wave_groups <= 1
        )
        if wave == 0:
            pl.semaphore_wait(barrier, trade_peers)

        def deal(step, carry):
            trade = partner(trade_peers - step)
            code_copy(wave, wave * trade_peers + trade, wave * trade_peers + my_trade, trade).start()
            unit_copy(wave, wave * trade_peers + trade, wave * trade_peers + my_trade, trade).start()
            return carry

        lax.fori_loop(1, trade_peers, deal, 0, unroll=unroll)
        mine = wave * trade_peers + my_trade
        code_recv[mine] = code_send[mine]
        unit_recv[mine] = unit_send[mine]

    member_ref[...] = jnp.transpose(member_wide).astype(jnp.bfloat16)
    gain_rows = jnp.concatenate(
        [jnp.broadcast_to(gains[d], (group_paths, trade_count)) for d in range(local_dates)], axis=0
    )
    gain_cols[...] = jnp.transpose(gain_rows)
    if groups > 2:
        total_ref[...] = jnp.zeros_like(total_ref)

    def order_rows(group, carry):
        rows = basis_ref[:, pl.ds(pl.multiple_of(group * group_paths, group_paths), group_paths), :]
        basis_rows[pl.ds(pl.multiple_of(group * group_rows, group_rows), group_rows), :] = (
            rows.reshape(group_rows, basis_count)
        )
        return carry

    lax.fori_loop(0, groups, order_rows, 0, unroll=groups <= 2)

    lags = lag_ref[...]
    first_core = my_date == 0

    def edge_copy(wave):
        return to_core(edge_send.at[wave], edge_recv.at[wave], edge_ss.at[wave], edge_rs.at[wave])

    for wave in range(WAVES):
        all_of(code_recv, code_ss.at[0], code_rs.at[wave], others).wait_recv()
        all_of(unit_recv, unit_ss.at[0], unit_rs.at[wave], others).wait_recv()

        def add(trade, total):
            source = wave * trade_peers + trade
            values = code_recv[source].astype(jnp.int32).astype(jnp.float32)
            return total + values * unit_recv[source]

        total = lax.fori_loop(
            0, trade_peers, add, jnp.zeros((chunk_rows, set_count), jnp.float32), unroll=unroll
        )
        edge_send[wave] = jnp.where(first_core, total[chunk_rows - edge_rows:], total[:edge_rows])
        edge_copy(wave).start()
        edge_copy(wave).wait_recv()
        edge = edge_recv[wave]
        before = jnp.where(first_core, 0.0, edge)
        netted = [before[i * own_paths:(i + 1) * own_paths] for i in range(LAG_MAX)]
        netted += [total[d * own_paths:(d + 1) * own_paths] for d in range(local_dates)]
        netted += [edge[i * own_paths:(i + 1) * own_paths] for i in range(LAG_MAX)]
        direct = []
        for d in range(LAG_MAX, len(netted)):
            value = netted[d]
            for lag in range(1, LAG_MAX + 1):
                value = value - jnp.where(lags == lag, netted[d - lag], 0.0)
            value = jnp.maximum(value - limit_ref[...], 0.0) * loss_scale
            if d >= LAG_MAX + local_dates:
                value = jnp.where(first_core, value, 0.0)
            direct.append(value)
        parts = []
        for d in range(local_dates):
            value = direct[d]
            for lag in range(1, LAG_MAX + 1):
                value = value - jnp.where(lags == lag, direct[d + lag], 0.0)
            parts.append(value)
        adj_send[wave] = jnp.concatenate(parts, axis=0).astype(jnp.bfloat16)

        def spread_out(step, carry):
            adj_copy(wave, wave, wave * trade_peers + my_trade, partner(trade_peers - step)).start()
            return carry

        lax.fori_loop(1, trade_peers, spread_out, 0, unroll=unroll)
        adj_recv[wave * trade_peers + my_trade] = adj_send[wave]

    def block_of(group):
        block = adj_recv[pl.ds(pl.multiple_of(group * GROUP, GROUP), GROUP)].astype(jnp.float32)
        block = block.reshape(GROUP, local_dates, own_paths, set_count)
        return jnp.concatenate(
            [block[i, d] for d in range(local_dates) for i in range(GROUP)], axis=0
        ).astype(jnp.bfloat16)

    piece_rows = trade_count // PIECES

    def gradient(group, block, first, count):
        rows = pl.ds(first, count)
        spread = lax.dot_general(member_ref[rows], block, NT, preferred_element_type=jnp.float32)
        scaled = (spread * gain_cols[rows]).astype(jnp.bfloat16)
        return jnp.dot(
            scaled, basis_rows[pl.ds(pl.multiple_of(group * group_rows, group_rows), group_rows), :],
            preferred_element_type=jnp.float32,
        )

    def keep(rows, part, fresh):
        for q in range(2):
            columns = part[:, q * half:(q + 1) * half]
            total_ref[q, rows] = columns if fresh else total_ref[q, rows] + columns

    def backward(group, carry):
        block = block_of(group)
        for piece in range(PIECES):
            part = gradient(group, block, piece * piece_rows, piece_rows)
            keep(pl.ds(piece * piece_rows, piece_rows), part, groups <= 2)
        return carry

    def half_copy(piece):
        rows = pl.ds(piece * piece_rows, piece_rows)
        return to_core(
            total_ref.at[1 - my_date, rows], half_recv.at[rows], half_ss.at[piece], half_rs.at[piece]
        )

    for wave in range(WAVES):
        all_of(adj_recv, adj_ss.at[0], adj_rs.at[wave], others).wait_recv()
        last = wave == WAVES - 1
        lax.fori_loop(
            wave * wave_groups, (wave + 1) * wave_groups - last, backward, 0, unroll=groups <= 2
        )

    last_block = block_of(groups - 1)
    for piece in range(PIECES):
        part = gradient(groups - 1, last_block, piece * piece_rows, piece_rows)
        keep(pl.ds(piece * piece_rows, piece_rows), part, False)
        half_copy(piece).start()

    all_of(code_send, code_ss.at[0], code_rs.at[0], WAVES * others).wait_send()
    all_of(unit_send, unit_ss.at[0], unit_rs.at[0], WAVES * others).wait_send()
    all_of(adj_recv, adj_ss.at[0], adj_rs.at[0], WAVES * others).wait_send()
    for wave in range(WAVES):
        edge_copy(wave).wait_send()
    for piece in range(PIECES):
        rows = pl.ds(piece * piece_rows, piece_rows)
        half_copy(piece).wait_recv()
        out_ref[rows] = total_ref[my_date, rows] + half_recv[rows]

    for piece in range(PIECES):
        half_copy(piece).wait_send()


def on_device(
    trade_peers, date_peers,
    basis_values, coefficients, set_map, trade_type, type_gain, set_lags, thresholds,
):
    local_dates, path_count, basis_count = basis_values.shape
    trade_count = coefficients.shape[0]
    set_count = thresholds.shape[0]
    slots = WAVES * trade_peers
    own_paths = path_count // slots
    chunk = local_dates * own_paths
    edge = LAG_MAX * own_paths
    group_rows = chunk * GROUP
    half = basis_count // 2
    loss_scale = 2.0 / math.sqrt(local_dates * date_peers * path_count)
    vmem_limit = min(60, 20 + 4 * local_dates * path_count // 512) * 1024 * 1024
    vmem = pl.BlockSpec(memory_space=pltpu.VMEM)
    dma = pltpu.SemaphoreType.DMA
    assert date_peers == 2 and local_dates >= LAG_MAX and trade_peers % GROUP == 0
    return pl.pallas_call(
        functools.partial(kernel, trade_peers, loss_scale),
        out_shape=jax.ShapeDtypeStruct((trade_count, half), jnp.float32),
        in_specs=[pl.BlockSpec(memory_space=pltpu.HBM)] * 7,
        out_specs=vmem,
        scratch_shapes=[
            pltpu.VMEM(type_gain.shape, jnp.float32),
            pltpu.VMEM(basis_values.shape, jnp.bfloat16),
            pltpu.VMEM(coefficients.shape, jnp.bfloat16),
            pltpu.VMEM((1, trade_count), jnp.int32),
            pltpu.VMEM((1, trade_count), jnp.int32),
            pltpu.VMEM((1, set_count), jnp.int32),
            pltpu.VMEM((1, set_count), jnp.float32),
            dma((7,)),
            pltpu.VMEM((slots, chunk, set_count), jnp.int16),
            pltpu.VMEM((slots, chunk, set_count), jnp.int16),
            pltpu.VMEM((slots, 1, set_count), jnp.float32),
            pltpu.VMEM((slots, 1, set_count), jnp.float32),
            pltpu.VMEM((WAVES, edge, set_count), jnp.float32),
            pltpu.VMEM((WAVES, edge, set_count), jnp.float32),
            pltpu.VMEM((WAVES, chunk, set_count), jnp.bfloat16),
            pltpu.VMEM((slots, chunk, set_count), jnp.bfloat16),
            pltpu.VMEM((trade_count, set_count), jnp.bfloat16),
            pltpu.VMEM((trade_count, group_rows), jnp.float32),
            pltpu.VMEM((path_count * local_dates, basis_count), jnp.bfloat16),
            pltpu.VMEM((2, trade_count, half), jnp.float32),
            pltpu.VMEM((trade_count, half), jnp.float32),
            dma((1,)), dma((WAVES,)), dma((1,)), dma((WAVES,)), dma((WAVES,)), dma((WAVES,)),
            dma((1,)), dma((WAVES,)), dma((PIECES,)), dma((PIECES,)),
        ],
        compiler_params=pltpu.CompilerParams(
            collective_id=0, has_side_effects=True, vmem_limit_bytes=vmem_limit
        ),
    )(
        *[
            pltpu.with_memory_space_constraint(x, pltpu.HBM)
            for x in (
                type_gain, basis_values, coefficients, set_map.reshape(1, -1),
                trade_type.reshape(1, -1), set_lags.reshape(1, -1), thresholds.reshape(1, -1),
            )
        ]
    )


def solution(mesh):
    return jax.shard_map(
        functools.partial(on_device, mesh.shape["trades"], mesh.shape["dates"]),
        mesh=mesh,
        in_specs=(
            P("dates", "groups", None),
            P("trades", None),
            P("trades"),
            P("trades"),
            P("dates", None),
            P(),
            P(),
        ),
        out_specs=P(("groups", "trades"), "dates"),
        check_vma=False,
    )
```

time: 23.9 us -> 23.3 us (0.975)
  Pallas kernels: 22.8 us -> 22.2 us
    pallas_call x1, Pallas kernels: 22.8 us -> 22.2 us  [on_device(): pl.pallas_call(functools.partial(kernel, trade_peers, loss_scale), out_sh...]
where the time goes in v2:
time: 23.3 us; the launch traced here: 23 us
  Pallas kernels  22.2 us (95%)
  local copies, waits for them, and re-layouts  0.8 us (3%)
    pallas_call x1, Pallas kernels, on_device(): pl.pallas_call(functools.partial(kernel, trade_peers, loss_scale), out_sh...  22.2 us
    unnamed x1, local copies, waits for them, and re-layouts  0.8 us

profile of v2, /device:TPU:1, one launch (start us, length us, event | category | flops | bytes accessed | tf_op | source)
XLA Modules:
  0.0 23.0 jit_solution(15745177887438960130)
XLA Ops:
  0.0 22.2 %shard_map.73 = f32[1024,128]{1,0:T(8,128)S(1)} custom-call(f32[4,16]{1,0:T(4,128)} %gain_in.1, bf16[4,128,256]{2,1,0:T(8,128)(2,1)} %basis_in.1, bf16[1024,256]{1,0:T(8,128)(2,1)} %coef_in.1, s32[1,1024]{1,0:T(1,128)} %bitcast.4, s32[1,1024]{1,0:T(1,128)} %bitcast.5, s32[1,256]{1,0:T(1,128)} %bitcast.6, f32[1,256]{1,0:T(1,128)} %bitcast.7), custom_call_target="tpu_custom_call" | custom-call | tf_op jit(solution)/shard_map/pallas_call | solution.py:305
  22.2 0.8 %copy.9 = f32[1024,128]{1,0:T(8,128)} copy(f32[1024,128]{1,0:T(8,128)S(1)} %shard_map.73) | data formatting | bytes 1048576

commit v3 on v2

v3 whole, which is shorter than its diff:
```python
import functools
import math

import jax
import jax.numpy as jnp
from jax import lax
from jax.experimental import pallas as pl
from jax.experimental.pallas import tpu as pltpu
from jax.sharding import PartitionSpec as P

LAG_MAX = 2
GROUP = 8
PIECES = 2
CODE_MAX = 32767.0
NT = (((1,), (1,)), ((), ()))


def kernel(
    trade_peers, loss_scale,
    gain_in, basis_in, coef_in, set_in, type_in, lag_in, limit_in,
    out_ref,
    gain_ref, basis_ref, coef_ref, set_ref, type_ref, lag_ref, limit_ref, load_sem,
    code_send, code_pass, code_recv, unit_send, unit_pass, unit_recv, gain_far, basis_far,
    adj_send, adj_recv, member_ref, gain_cols, basis_rows, total_ref, half_recv,
    code_ss, code_rs, unit_ss, unit_rs, pass_ss, pass_rs, adj_ss, adj_rs, half_ss, half_rs,
):
    my_trade = lax.axis_index("trades")
    my_core = lax.axis_index("dates")
    other_core = 1 - my_core
    local_dates, path_count, basis_count = basis_ref.shape
    trade_count = coef_ref.shape[0]
    set_count = limit_ref.shape[1]
    type_count = gain_ref.shape[1]
    others = trade_peers - 1
    core_paths = path_count // 2
    own_paths = core_paths // trade_peers
    core_groups = trade_peers // GROUP
    group_paths = GROUP * own_paths
    group_rows = local_dates * group_paths
    chunk_rows = local_dates * own_paths
    half = basis_count // 2
    unroll = trade_peers <= 8

    def partner(step):
        trade = 0
        for bit in range(others.bit_length()):
            weight = 2 ** bit
            mine = (my_trade // weight) % 2
            flip = (step // weight) % 2
            trade += weight * (mine + flip - 2 * mine * flip)
        return trade

    barrier = pltpu.get_barrier_semaphore()

    def greet(step, carry):
        pl.semaphore_signal(
            barrier, inc=1, device_id={"trades": partner(trade_peers - step)},
            device_id_type=pl.DeviceIdType.MESH,
        )
        return carry

    lax.fori_loop(1, trade_peers, greet, 0, unroll=unroll)
    pl.semaphore_signal(
        barrier, inc=1, device_id={"dates": other_core}, device_id_type=pl.DeviceIdType.MESH
    )
    loads = [
        pltpu.make_async_copy(source, target, load_sem.at[i])
        for i, (source, target) in enumerate((
            (type_in, type_ref), (gain_in, gain_ref), (set_in, set_ref), (basis_in, basis_ref),
            (coef_in, coef_ref), (lag_in, lag_ref), (limit_in, limit_ref),
        ))
    ]
    for load in loads:
        load.start()
    for load in loads[:3]:
        load.wait()

    def to_trade(source, target, send_sem, recv_sem, trade):
        return pltpu.make_async_remote_copy(
            src_ref=source, dst_ref=target, send_sem=send_sem, recv_sem=recv_sem,
            device_id={"trades": trade}, device_id_type=pl.DeviceIdType.MESH,
        )

    def to_core(source, target, send_sem, recv_sem):
        return pltpu.make_async_remote_copy(
            src_ref=source, dst_ref=target, send_sem=send_sem, recv_sem=recv_sem,
            device_id={"dates": other_core}, device_id_type=pl.DeviceIdType.MESH,
        )

    def all_of(buffer, send_sem, recv_sem, count):
        slots = buffer.at[pl.ds(0, count)]
        return to_trade(slots, slots, send_sem, recv_sem, my_trade)

    types = type_ref[...]

    def gains_of(table):
        gains = []
        for d in range(local_dates):
            row = jnp.zeros_like(types, dtype=jnp.float32)
            for y in range(type_count):
                row = jnp.where(types == y, table[d:d + 1, y:y + 1], row)
            gains.append(row)
        return gains

    gains = gains_of(gain_ref[...])
    set_ids = lax.broadcasted_iota(jnp.int32, (set_count, trade_count), 0)
    member_wide = jnp.where(set_ids == set_ref[...], 1.0, 0.0)
    member = member_wide.astype(jnp.bfloat16)

    for load in loads[3:]:
        load.wait()

    def forward(group, carry):
        rows = basis_ref[:, pl.ds(pl.multiple_of(group * group_paths, group_paths), group_paths), :]
        raw = lax.dot_general(
            rows.reshape(group_rows, basis_count), coef_ref[...], NT,
            preferred_element_type=jnp.float32,
        )
        prices = jnp.concatenate(
            [raw[d * group_paths:(d + 1) * group_paths] * gains[d] for d in range(local_dates)], axis=0
        ).astype(jnp.bfloat16)
        part = lax.dot_general(prices, member, NT, preferred_element_type=jnp.float32)
        part = part.reshape(local_dates, GROUP, own_paths, set_count)
        for i in range(GROUP):
            chunk = part[:, i].reshape(chunk_rows, set_count)
            top = jnp.maximum(jnp.max(jnp.abs(chunk), axis=0, keepdims=True), 1e-30)
            codes = jnp.round(chunk * (CODE_MAX / top)).astype(jnp.int32)
            code_send[group * GROUP + i] = codes.astype(jnp.int16)
            unit_send[group * GROUP + i] = top * (1.0 / CODE_MAX)

        return carry

    lax.fori_loop(0, 2 * core_groups, forward, 0, unroll=core_groups <= 1)
    pl.semaphore_wait(barrier, trade_peers)
    theirs = pl.ds(other_core * trade_peers, trade_peers)
    their_paths = pl.ds(pl.multiple_of(other_core * core_paths, core_paths), core_paths)
    code_over = to_core(code_send.at[theirs], code_pass, pass_ss.at[0], pass_rs.at[0])
    unit_over = to_core(unit_send.at[theirs], unit_pass, pass_ss.at[1], pass_rs.at[1])
    gain_over = to_core(gain_ref, gain_far, pass_ss.at[2], pass_rs.at[2])
    basis_over = to_core(basis_ref.at[:, their_paths], basis_far, pass_ss.at[3], pass_rs.at[3])
    code_over.start()
    unit_over.start()

    def deal(codes, units, first, dates):
        def one(step, carry):
            trade = partner(trade_peers - step)
            slot = dates * trade_peers + my_trade
            to_trade(
                codes.at[first + trade], code_recv.at[slot], code_ss.at[0], code_rs.at[0], trade
            ).start()
            to_trade(
                units.at[first + trade], unit_recv.at[slot], unit_ss.at[0], unit_rs.at[0], trade
            ).start()
            return carry

        lax.fori_loop(1, trade_peers, one, 0, unroll=unroll)

    mine = my_core * trade_peers
    deal(code_send, unit_send, mine, my_core)
    code_recv[mine + my_trade] = code_send[mine + my_trade]
    unit_recv[mine + my_trade] = unit_send[mine + my_trade]
    member_ref[...] = jnp.transpose(member_wide).astype(jnp.bfloat16)
    code_over.wait_recv()
    unit_over.wait_recv()
    deal(code_pass, unit_pass, 0, other_core)
    gain_over.start()
    basis_over.start()
    far = other_core * trade_peers
    code_recv[far + my_trade] = code_pass[my_trade]
    unit_recv[far + my_trade] = unit_pass[my_trade]

    def widen(gains, dates):
        wide = jnp.concatenate(
            [jnp.broadcast_to(gains[d], (group_paths, trade_count)) for d in range(local_dates)], axis=0
        )
        gain_cols[dates] = jnp.transpose(wide)

    def order_rows(source, first, dates):
        def one(group, carry):
            start = pl.multiple_of(first + group * group_paths, group_paths)
            basis_rows[dates * core_groups + group] = (
                source[:, pl.ds(start, group_paths), :].reshape(group_rows, basis_count)
            )
            return carry

        lax.fori_loop(0, core_groups, one, 0, unroll=core_groups <= 1)

    widen(gains, my_core)
    order_rows(basis_ref, my_core * core_paths, my_core)
    if core_groups > 1:
        total_ref[...] = jnp.zeros_like(total_ref)

    all_of(code_recv, code_ss.at[0], code_rs.at[0], 2 * others).wait_recv()
    all_of(unit_recv, unit_ss.at[0], unit_rs.at[0], 2 * others).wait_recv()

    def add(trade, totals):
        result = []
        for q in range(2):
            source = q * trade_peers + trade
            values = code_recv[source].astype(jnp.int32).astype(jnp.float32)
            result.append(totals[q] + values * unit_recv[source])
        return tuple(result)

    totals = lax.fori_loop(
        0, trade_peers, add,
        tuple(jnp.zeros((chunk_rows, set_count), jnp.float32) for _ in range(2)), unroll=unroll,
    )
    netted = [
        totals[q][d * own_paths:(d + 1) * own_paths] for q in range(2) for d in range(local_dates)
    ]
    date_count = len(netted)
    lags = lag_ref[...]
    direct = []
    for d in range(date_count):
        value = netted[d]
        for lag in range(1, LAG_MAX + 1):
            if d >= lag:
                value = value - jnp.where(lags == lag, netted[d - lag], 0.0)
        direct.append(jnp.maximum(value - limit_ref[...], 0.0) * loss_scale)
    for q in range(2):
        parts = []
        for d in range(q * local_dates, (q + 1) * local_dates):
            value = direct[d]
            for lag in range(1, LAG_MAX + 1):
                if d + lag < date_count:
                    value = value - jnp.where(lags == lag, direct[d + lag], 0.0)
            parts.append(value)
        adj_send[q] = jnp.concatenate(parts, axis=0).astype(jnp.bfloat16)

    for q in range(2):
        def spread_out(step, carry):
            trade = partner(trade_peers - step)
            to_trade(
                adj_send.at[q], adj_recv.at[q * trade_peers + my_trade], adj_ss.at[0], adj_rs.at[q], trade
            ).start()
            return carry

        lax.fori_loop(1, trade_peers, spread_out, 0, unroll=unroll)
        adj_recv[q * trade_peers + my_trade] = adj_send[q]

    gain_over.wait_recv()
    basis_over.wait_recv()
    widen(gains_of(gain_far[...]), other_core)
    order_rows(basis_far, 0, other_core)

    def block_of(group):
        block = adj_recv[pl.ds(pl.multiple_of(group * GROUP, GROUP), GROUP)].astype(jnp.float32)
        block = block.reshape(GROUP, local_dates, own_paths, set_count)
        return jnp.concatenate(
            [block[i, d] for d in range(local_dates) for i in range(GROUP)], axis=0
        ).astype(jnp.bfloat16)

    piece_rows = trade_count // PIECES

    def gradient(dates, group, block, piece):
        rows = pl.ds(piece * piece_rows, piece_rows)
        spread = lax.dot_general(member_ref[rows], block, NT, preferred_element_type=jnp.float32)
        scaled = (spread * gain_cols[dates, rows]).astype(jnp.bfloat16)
        return jnp.dot(scaled, basis_rows[group], preferred_element_type=jnp.float32)

    def keep(piece, part, fresh):
        rows = pl.ds(piece * piece_rows, piece_rows)
        for q in range(2):
            columns = part[:, q * half:(q + 1) * half]
            total_ref[q, rows] = columns if fresh else total_ref[q, rows] + columns

    def half_copy(piece):
        rows = pl.ds(piece * piece_rows, piece_rows)
        return to_core(
            total_ref.at[other_core, rows], half_recv.at[rows], half_ss.at[piece], half_rs.at[piece]
        )

    for dates in range(2):
        def backward(group, carry):
            block = block_of(group)
            for piece in range(PIECES):
                keep(piece, gradient(dates, group, block, piece), core_groups == 1)
            return carry

        all_of(adj_recv, adj_ss.at[0], adj_rs.at[dates], others).wait_recv()
        lax.fori_loop(
            dates * core_groups, (dates + 1) * core_groups - dates, backward, 0,
            unroll=core_groups <= 1,
        )

    final = 2 * core_groups - 1
    block = block_of(final)
    for piece in range(PIECES):
        keep(piece, gradient(1, final, block, piece), False)
        half_copy(piece).start()

    all_of(code_send, code_ss.at[0], code_rs.at[0], 2 * others).wait_send()
    all_of(unit_send, unit_ss.at[0], unit_rs.at[0], 2 * others).wait_send()
    all_of(adj_recv, adj_ss.at[0], adj_rs.at[0], 2 * others).wait_send()
    for copy in (code_over, unit_over, gain_over, basis_over):
        copy.wait_send()
    for piece in range(PIECES):
        rows = pl.ds(piece * piece_rows, piece_rows)
        half_copy(piece).wait_recv()
        out_ref[rows] = total_ref[my_core, rows] + half_recv[rows]

    for piece in range(PIECES):
        half_copy(piece).wait_send()


def on_device(
    trade_peers, date_peers,
    basis_values, coefficients, set_map, trade_type, type_gain, set_lags, thresholds,
):
    local_dates, path_count, basis_count = basis_values.shape
    trade_count = coefficients.shape[0]
    set_count = thresholds.shape[0]
    slots = 2 * trade_peers
    chunk = local_dates * path_count // slots
    group_rows = chunk * GROUP
    half = basis_count // 2
    loss_scale = 2.0 / math.sqrt(local_dates * date_peers * path_count)
    vmem_limit = min(60, 20 + 4 * local_dates * path_count // 512) * 1024 * 1024
    vmem = pl.BlockSpec(memory_space=pltpu.VMEM)
    dma = pltpu.SemaphoreType.DMA
    assert date_peers == 2 and trade_peers % GROUP == 0
    return pl.pallas_call(
        functools.partial(kernel, trade_peers, loss_scale),
        out_shape=jax.ShapeDtypeStruct((trade_count, half), jnp.float32),
        in_specs=[pl.BlockSpec(memory_space=pltpu.HBM)] * 7,
        out_specs=vmem,
        scratch_shapes=[
            pltpu.VMEM(type_gain.shape, jnp.float32),
            pltpu.VMEM(basis_values.shape, jnp.bfloat16),
            pltpu.VMEM(coefficients.shape, jnp.bfloat16),
            pltpu.VMEM((1, trade_count), jnp.int32),
            pltpu.VMEM((1, trade_count), jnp.int32),
            pltpu.VMEM((1, set_count), jnp.int32),
            pltpu.VMEM((1, set_count), jnp.float32),
            dma((7,)),
            pltpu.VMEM((slots, chunk, set_count), jnp.int16),
            pltpu.VMEM((trade_peers, chunk, set_count), jnp.int16),
            pltpu.VMEM((slots, chunk, set_count), jnp.int16),
            pltpu.VMEM((slots, 1, set_count), jnp.float32),
            pltpu.VMEM((trade_peers, 1, set_count), jnp.float32),
            pltpu.VMEM((slots, 1, set_count), jnp.float32),
            pltpu.VMEM(type_gain.shape, jnp.float32),
            pltpu.VMEM((local_dates, path_count // 2, basis_count), jnp.bfloat16),
            pltpu.VMEM((2, chunk, set_count), jnp.bfloat16),
            pltpu.VMEM((slots, chunk, set_count), jnp.bfloat16),
            pltpu.VMEM((trade_count, set_count), jnp.bfloat16),
            pltpu.VMEM((2, trade_count, group_rows), jnp.float32),
            pltpu.VMEM((slots // GROUP, group_rows, basis_count), jnp.bfloat16),
            pltpu.VMEM((2, trade_count, half), jnp.float32),
            pltpu.VMEM((trade_count, half), jnp.float32),
            dma((1,)), dma((1,)), dma((1,)), dma((1,)), dma((4,)), dma((4,)),
            dma((1,)), dma((2,)), dma((PIECES,)), dma((PIECES,)),
        ],
        compiler_params=pltpu.CompilerParams(
            collective_id=0, has_side_effects=True, vmem_limit_bytes=vmem_limit
        ),
    )(
        *[
            pltpu.with_memory_space_constraint(x, pltpu.HBM)
            for x in (
                type_gain, basis_values, coefficients, set_map.reshape(1, -1),
                trade_type.reshape(1, -1), set_lags.reshape(1, -1), thresholds.reshape(1, -1),
            )
        ]
    )


def solution(mesh):
    return jax.shard_map(
        functools.partial(on_device, mesh.shape["trades"], mesh.shape["dates"]),
        mesh=mesh,
        in_specs=(
            P("dates", "groups", None),
            P("trades", None),
            P("trades"),
            P("trades"),
            P("dates", None),
            P(),
            P(),
        ),
        out_specs=P(("groups", "trades"), "dates"),
        check_vma=False,
    )
```

time: 23.3 us -> 23.4 us (level)
  no operation moved by 1% of the time
where the time goes in v3:
time: 23.4 us; the launch traced here: 23.2 us
  Pallas kernels  22.4 us (96%)
  local copies, waits for them, and re-layouts  0.8 us (3%)
    pallas_call x1, Pallas kernels, on_device(): pl.pallas_call(functools.partial(kernel, trade_peers, loss_scale), out_sh...  22.4 us
    unnamed x1, local copies, waits for them, and re-layouts  0.8 us

profile of v3, /device:TPU:1, one launch (start us, length us, event | category | flops | bytes accessed | tf_op | source)
XLA Modules:
  0.0 23.2 jit_solution(16286487183446697696)
XLA Ops:
  0.0 22.4 %shard_map.73 = f32[1024,128]{1,0:T(8,128)S(1)} custom-call(f32[4,16]{1,0:T(4,128)} %gain_in.1, bf16[4,128,256]{2,1,0:T(8,128)(2,1)} %basis_in.1, bf16[1024,256]{1,0:T(8,128)(2,1)} %coef_in.1, s32[1,1024]{1,0:T(1,128)} %bitcast.4, s32[1,1024]{1,0:T(1,128)} %bitcast.5, s32[1,256]{1,0:T(1,128)} %bitcast.6, f32[1,256]{1,0:T(1,128)} %bitcast.7), custom_call_target="tpu_custom_call" | custom-call | tf_op jit(solution)/shard_map/pallas_call | solution.py:322
  22.4 0.8 %copy.9 = f32[1024,128]{1,0:T(8,128)} copy(f32[1024,128]{1,0:T(8,128)S(1)} %shard_map.73) | data formatting | bytes 1048576

commit v4 on v3

--- a/solution.py
+++ b/solution.py
@@ -22,7 +22,7 @@
     gain_ref, basis_ref, coef_ref, set_ref, type_ref, lag_ref, limit_ref, load_sem,
     code_send, code_pass, code_recv, unit_send, unit_pass, unit_recv, gain_far, basis_far,
     adj_send, adj_recv, member_ref, gain_cols, basis_rows, total_ref, half_recv,
-    code_ss, code_rs, unit_ss, unit_rs, pass_ss, pass_rs, adj_ss, adj_rs, half_ss, half_rs,
+    code_ss, code_rs, unit_ss, unit_rs, pass_ss, pass_rs, adj_ss, adj_rs, cross_rs, half_ss, half_rs,
 ):
     my_trade = lax.axis_index("trades")
     my_core = lax.axis_index("dates")
@@ -227,21 +227,52 @@
             parts.append(value)
         adj_send[q] = jnp.concatenate(parts, axis=0).astype(jnp.bfloat16)
 
+    forwards = my_core == 1
+    neighbour = partner(1)
+    pairs = trade_peers // 2
+
+    def adj_copy(q, trade, sems):
+        return to_trade(
+            adj_send.at[q], adj_recv.at[q * trade_peers + my_trade], adj_ss.at[0], sems.at[q], trade
+        )
+
     for q in range(2):
-        def spread_out(step, carry):
-            trade = partner(trade_peers - step)
-            to_trade(
-                adj_send.at[q], adj_recv.at[q * trade_peers + my_trade], adj_ss.at[0], adj_rs.at[q], trade
-            ).start()
+        def spread_out(pair, carry):
+            @pl.when(jnp.logical_not(forwards))
+            def _():
+                adj_copy(q, partner(trade_peers + 1 - 2 * pair), cross_rs).start()
+
+            adj_copy(q, partner(trade_peers - 2 * pair), adj_rs).start()
             return carry
 
-        lax.fori_loop(1, trade_peers, spread_out, 0, unroll=unroll)
+        lax.fori_loop(1, pairs, spread_out, 0, unroll=unroll)
+        adj_copy(q, neighbour, cross_rs).start()
         adj_recv[q * trade_peers + my_trade] = adj_send[q]
 
     gain_over.wait_recv()
     basis_over.wait_recv()
     widen(gains_of(gain_far[...]), other_core)
     order_rows(basis_far, 0, other_core)
+
+    def column_arrived(q):
+        all_of(adj_recv, adj_ss.at[0], adj_rs.at[q], pairs - 1).wait_recv()
+
+    @pl.when(forwards)
+    def _():
+        for q in range(2):
+            column_arrived(q)
+
+            def forward_block(pair, carry):
+                block = adj_recv.at[q * trade_peers + partner(trade_peers - 2 * pair)]
+                to_trade(block, block, adj_ss.at[0], cross_rs.at[q], neighbour).start()
+                return carry
+
+            lax.fori_loop(1, pairs, forward_block, 0, unroll=unroll)
+
+    @pl.when(jnp.logical_not(forwards))
+    def _():
+        for q in range(2):
+            column_arrived(q)
 
     def block_of(group):
         block = adj_recv[pl.ds(pl.multiple_of(group * GROUP, GROUP), GROUP)].astype(jnp.float32)
@@ -277,7 +308,7 @@
                 keep(piece, gradient(dates, group, block, piece), core_groups == 1)
             return carry
 
-        all_of(adj_recv, adj_ss.at[0], adj_rs.at[dates], others).wait_recv()
+        all_of(adj_recv, adj_ss.at[0], cross_rs.at[dates], pairs).wait_recv()
         lax.fori_loop(
             dates * core_groups, (dates + 1) * core_groups - dates, backward, 0,
             unroll=core_groups <= 1,
@@ -349,7 +380,7 @@
             pltpu.VMEM((2, trade_count, half), jnp.float32),
             pltpu.VMEM((trade_count, half), jnp.float32),
             dma((1,)), dma((1,)), dma((1,)), dma((1,)), dma((4,)), dma((4,)),
-            dma((1,)), dma((2,)), dma((PIECES,)), dma((PIECES,)),
+            dma((1,)), dma((2,)), dma((2,)), dma((PIECES,)), dma((PIECES,)),
         ],
         compiler_params=pltpu.CompilerParams(
             collective_id=0, has_side_effects=True, vmem_limit_bytes=vmem_limit

time: 23.4 us -> 23.2 us (level)
  Pallas kernels: 22.4 us -> 22.1 us
    pallas_call x1, Pallas kernels: 22.4 us -> 22.1 us  [on_device(): pl.pallas_call(functools.partial(kernel, trade_peers, loss_scale), out_sh...]
where the time goes in v4:
time: 23.2 us; the launch traced here: 22.9 us
  Pallas kernels  22.1 us (95%)
  local copies, waits for them, and re-layouts  0.8 us (3%)
    pallas_call x1, Pallas kernels, on_device(): pl.pallas_call(functools.partial(kernel, trade_peers, loss_scale), out_sh...  22.1 us
    unnamed x1, local copies, waits for them, and re-layouts  0.8 us

profile of v4, /device:TPU:1, one launch (start us, length us, event | category | flops | bytes accessed | tf_op | source)
XLA Modules:
  0.0 22.9 jit_solution(14735128913637138983)
XLA Ops:
  0.0 22.1 %shard_map.73 = f32[1024,128]{1,0:T(8,128)S(1)} custom-call(f32[4,16]{1,0:T(4,128)} %gain_in.1, bf16[4,128,256]{2,1,0:T(8,128)(2,1)} %basis_in.1, bf16[1024,256]{1,0:T(8,128)(2,1)} %coef_in.1, s32[1,1024]{1,0:T(1,128)} %bitcast.4, s32[1,1024]{1,0:T(1,128)} %bitcast.5, s32[1,256]{1,0:T(1,128)} %bitcast.6, f32[1,256]{1,0:T(1,128)} %bitcast.7), custom_call_target="tpu_custom_call" | custom-call | tf_op jit(solution)/shard_map/pallas_call | solution.py:353
  22.1 0.8 %copy.9 = f32[1024,128]{1,0:T(8,128)} copy(f32[1024,128]{1,0:T(8,128)S(1)} %shard_map.73) | data formatting | bytes 1048576

commit v5 on v3

--- a/solution.py
+++ b/solution.py
@@ -10,7 +10,8 @@
 
 LAG_MAX = 2
 GROUP = 8
-PIECES = 2
+SPAN = 4
+PIECES = 4
 CODE_MAX = 32767.0
 NT = (((1,), (1,)), ((), ()))
 
@@ -21,7 +22,7 @@
     out_ref,
     gain_ref, basis_ref, coef_ref, set_ref, type_ref, lag_ref, limit_ref, load_sem,
     code_send, code_pass, code_recv, unit_send, unit_pass, unit_recv, gain_far, basis_far,
-    adj_send, adj_recv, member_ref, gain_cols, basis_rows, total_ref, half_recv,
+    adj_send, adj_recv, member_ref, gain_cols, basis_rows, scaled_ref, total_ref, half_recv,
     code_ss, code_rs, unit_ss, unit_rs, pass_ss, pass_rs, adj_ss, adj_rs, half_ss, half_rs,
 ):
     my_trade = lax.axis_index("trades")
@@ -38,6 +39,9 @@
     group_paths = GROUP * own_paths
     group_rows = local_dates * group_paths
     chunk_rows = local_dates * own_paths
+    spans = trade_peers // SPAN
+    span_paths = SPAN * own_paths
+    half_rows = local_dates * span_paths
     half = basis_count // 2
     unroll = trade_peers <= 8
 
@@ -171,23 +175,24 @@
 
     def widen(gains, dates):
         wide = jnp.concatenate(
-            [jnp.broadcast_to(gains[d], (group_paths, trade_count)) for d in range(local_dates)], axis=0
-        )
-        gain_cols[dates] = jnp.transpose(wide)
+            [jnp.broadcast_to(gains[d], (span_paths, trade_count)) for d in range(local_dates)], axis=0
+        )
+        columns = pl.ds(pl.multiple_of(dates * half_rows, half_rows), half_rows)
+        gain_cols[:, columns] = jnp.transpose(wide)
 
     def order_rows(source, first, dates):
-        def one(group, carry):
-            start = pl.multiple_of(first + group * group_paths, group_paths)
-            basis_rows[dates * core_groups + group] = (
-                source[:, pl.ds(start, group_paths), :].reshape(group_rows, basis_count)
+        def one(span, carry):
+            start = pl.multiple_of(first + span * span_paths, span_paths)
+            basis_rows[span, dates] = (
+                source[:, pl.ds(start, span_paths), :].reshape(half_rows, basis_count)
             )
             return carry
 
-        lax.fori_loop(0, core_groups, one, 0, unroll=core_groups <= 1)
+        lax.fori_loop(0, spans, one, 0, unroll=spans <= 2)
 
     widen(gains, my_core)
     order_rows(basis_ref, my_core * core_paths, my_core)
-    if core_groups > 1:
+    if spans > 2:
         total_ref[...] = jnp.zeros_like(total_ref)
 
     all_of(code_recv, code_ss.at[0], code_rs.at[0], 2 * others).wait_recv()
@@ -217,52 +222,60 @@
             if d >= lag:
                 value = value - jnp.where(lags == lag, netted[d - lag], 0.0)
         direct.append(jnp.maximum(value - limit_ref[...], 0.0) * loss_scale)
-    for q in range(2):
-        parts = []
-        for d in range(q * local_dates, (q + 1) * local_dates):
-            value = direct[d]
-            for lag in range(1, LAG_MAX + 1):
-                if d + lag < date_count:
-                    value = value - jnp.where(lags == lag, direct[d + lag], 0.0)
-            parts.append(value)
-        adj_send[q] = jnp.concatenate(parts, axis=0).astype(jnp.bfloat16)
-
-    for q in range(2):
-        def spread_out(step, carry):
-            trade = partner(trade_peers - step)
-            to_trade(
-                adj_send.at[q], adj_recv.at[q * trade_peers + my_trade], adj_ss.at[0], adj_rs.at[q], trade
-            ).start()
-            return carry
-
-        lax.fori_loop(1, trade_peers, spread_out, 0, unroll=unroll)
-        adj_recv[q * trade_peers + my_trade] = adj_send[q]
+    parts = []
+    for d in range(date_count):
+        value = direct[d]
+        for lag in range(1, LAG_MAX + 1):
+            if d + lag < date_count:
+                value = value - jnp.where(lags == lag, direct[d + lag], 0.0)
+        parts.append(value)
+    adj_send[...] = jnp.concatenate(parts, axis=0).astype(jnp.bfloat16)
+
+    side = trade_peers // 2
+    my_side = my_trade // side
+
+    def adj_copy(trade):
+        far = my_side + trade // side - 2 * my_side * (trade // side)
+        return to_trade(adj_send, adj_recv.at[my_trade], adj_ss.at[0], adj_rs.at[far], trade)
+
+    def spread_out(step, carry):
+        adj_copy(step + (step + trade_peers - my_trade) // trade_peers).start()
+        return carry
+
+    lax.fori_loop(0, others, spread_out, 0, unroll=unroll)
+    adj_recv[my_trade] = adj_send[...]
 
     gain_over.wait_recv()
     basis_over.wait_recv()
     widen(gains_of(gain_far[...]), other_core)
     order_rows(basis_far, 0, other_core)
 
-    def block_of(group):
-        block = adj_recv[pl.ds(pl.multiple_of(group * GROUP, GROUP), GROUP)].astype(jnp.float32)
-        block = block.reshape(GROUP, local_dates, own_paths, set_count)
+    def block_of(span):
+        block = adj_recv[pl.ds(span * SPAN, SPAN)].astype(jnp.float32)
+        block = block.reshape(SPAN, date_count, own_paths, set_count)
         return jnp.concatenate(
-            [block[i, d] for d in range(local_dates) for i in range(GROUP)], axis=0
+            [block[i, d] for d in range(date_count) for i in range(SPAN)], axis=0
         ).astype(jnp.bfloat16)
 
-    piece_rows = trade_count // PIECES
-
-    def gradient(dates, group, block, piece):
-        rows = pl.ds(piece * piece_rows, piece_rows)
-        spread = lax.dot_general(member_ref[rows], block, NT, preferred_element_type=jnp.float32)
-        scaled = (spread * gain_cols[dates, rows]).astype(jnp.bfloat16)
-        return jnp.dot(scaled, basis_rows[group], preferred_element_type=jnp.float32)
-
-    def keep(piece, part, fresh):
-        rows = pl.ds(piece * piece_rows, piece_rows)
+    def scaled_of(span):
+        spread = lax.dot_general(
+            member_ref[...], block_of(span), NT, preferred_element_type=jnp.float32
+        )
+        return (spread * gain_cols[...]).astype(jnp.bfloat16)
+
+    def gradient(span, scaled):
+        rows = basis_rows[span].reshape(2 * half_rows, basis_count)
+        return jnp.dot(scaled, rows, preferred_element_type=jnp.float32)
+
+    def backward(step, carry):
+        span = lax.rem(my_side * (spans // 2) + step, spans)
+        part = gradient(span, scaled_of(span))
         for q in range(2):
             columns = part[:, q * half:(q + 1) * half]
-            total_ref[q, rows] = columns if fresh else total_ref[q, rows] + columns
+            total_ref[q] = columns if spans <= 2 else total_ref[q] + columns
+        return carry
+
+    piece_rows = trade_count // PIECES
 
     def half_copy(piece):
         rows = pl.ds(piece * piece_rows, piece_rows)
@@ -270,28 +283,22 @@
             total_ref.at[other_core, rows], half_recv.at[rows], half_ss.at[piece], half_rs.at[piece]
         )
 
-    for dates in range(2):
-        def backward(group, carry):
-            block = block_of(group)
-            for piece in range(PIECES):
-                keep(piece, gradient(dates, group, block, piece), core_groups == 1)
-            return carry
-
-        all_of(adj_recv, adj_ss.at[0], adj_rs.at[dates], others).wait_recv()
-        lax.fori_loop(
-            dates * core_groups, (dates + 1) * core_groups - dates, backward, 0,
-            unroll=core_groups <= 1,
-        )
-
-    final = 2 * core_groups - 1
-    block = block_of(final)
+    all_of(adj_recv, adj_ss.at[0], adj_rs.at[0], side - 1).wait_recv()
+    lax.fori_loop(0, spans // 2, backward, 0, unroll=spans <= 2)
+    all_of(adj_recv, adj_ss.at[0], adj_rs.at[1], side).wait_recv()
+    lax.fori_loop(spans // 2, spans - 1, backward, 0, unroll=spans <= 2)
+    final = lax.rem(my_side * (spans // 2) + spans - 1, spans)
+    scaled_ref[...] = scaled_of(final)
     for piece in range(PIECES):
-        keep(piece, gradient(1, final, block, piece), False)
+        rows = pl.ds(piece * piece_rows, piece_rows)
+        part = gradient(final, scaled_ref[rows])
+        for q in range(2):
+            total_ref[q, rows] += part[:, q * half:(q + 1) * half]
         half_copy(piece).start()
 
     all_of(code_send, code_ss.at[0], code_rs.at[0], 2 * others).wait_send()
     all_of(unit_send, unit_ss.at[0], unit_rs.at[0], 2 * others).wait_send()
-    all_of(adj_recv, adj_ss.at[0], adj_rs.at[0], 2 * others).wait_send()
+    all_of(adj_recv, adj_ss.at[0], adj_rs.at[0], others).wait_send()
     for copy in (code_over, unit_over, gain_over, basis_over):
         copy.wait_send()
     for piece in range(PIECES):
@@ -312,13 +319,13 @@
     set_count = thresholds.shape[0]
     slots = 2 * trade_peers
     chunk = local_dates * path_count // slots
-    group_rows = chunk * GROUP
+    half_rows = chunk * SPAN
     half = basis_count // 2
     loss_scale = 2.0 / math.sqrt(local_dates * date_peers * path_count)
     vmem_limit = min(60, 20 + 4 * local_dates * path_count // 512) * 1024 * 1024
     vmem = pl.BlockSpec(memory_space=pltpu.VMEM)
     dma = pltpu.SemaphoreType.DMA
-    assert date_peers == 2 and trade_peers % GROUP == 0
+    assert date_peers == 2 and trade_peers % GROUP == 0 and trade_peers % (2 * SPAN) == 0
     return pl.pallas_call(
         functools.partial(kernel, trade_peers, loss_scale),
         out_shape=jax.ShapeDtypeStruct((trade_count, half), jnp.float32),
@@ -341,11 +348,12 @@
             pltpu.VMEM((slots, 1, set_count), jnp.float32),
             pltpu.VMEM(type_gain.shape, jnp.float32),
             pltpu.VMEM((local_dates, path_count // 2, basis_count), jnp.bfloat16),
-            pltpu.VMEM((2, chunk, set_count), jnp.bfloat16),
-            pltpu.VMEM((slots, chunk, set_count), jnp.bfloat16),
+            pltpu.VMEM((2 * chunk, set_count), jnp.bfloat16),
+            pltpu.VMEM((trade_peers, 2 * chunk, set_count), jnp.bfloat16),
             pltpu.VMEM((trade_count, set_count), jnp.bfloat16),
-            pltpu.VMEM((2, trade_count, group_rows), jnp.float32),
-            pltpu.VMEM((slots // GROUP, group_rows, basis_count), jnp.bfloat16),
+            pltpu.VMEM((trade_count, 2 * half_rows), jnp.float32),
+            pltpu.VMEM((trade_peers // SPAN, 2, half_rows, basis_count), jnp.bfloat16),
+            pltpu.VMEM((trade_count, 2 * half_rows), jnp.bfloat16),
             pltpu.VMEM((2, trade_count, half), jnp.float32),
             pltpu.VMEM((trade_count, half), jnp.float32),
             dma((1,)), dma((1,)), dma((1,)), dma((1,)), dma((4,)), dma((4,)),

time: 23.4 us -> 21.8 us (0.932)
  Pallas kernels: 22.4 us -> 20.7 us
    pallas_call x1, Pallas kernels: 22.4 us -> 20.7 us  [on_device(): pl.pallas_call(functools.partial(kernel, trade_peers, loss_scale), out_sh...]
where the time goes in v5:
time: 21.8 us; the launch traced here: 21.5 us
  Pallas kernels  20.7 us (95%)
  local copies, waits for them, and re-layouts  0.8 us (4%)
    pallas_call x1, Pallas kernels, on_device(): pl.pallas_call(functools.partial(kernel, trade_peers, loss_scale), out_sh...  20.7 us
    unnamed x1, local copies, waits for them, and re-layouts  0.8 us

profile of v5, /device:TPU:1, one launch (start us, length us, event | category | flops | bytes accessed | tf_op | source)
XLA Modules:
  0.0 21.5 jit_solution(14162891296357748609)
XLA Ops:
  0.0 20.7 %shard_map.73 = f32[1024,128]{1,0:T(8,128)S(1)} custom-call(f32[4,16]{1,0:T(4,128)} %gain_in.1, bf16[4,128,256]{2,1,0:T(8,128)(2,1)} %basis_in.1, bf16[1024,256]{1,0:T(8,128)(2,1)} %coef_in.1, s32[1,1024]{1,0:T(1,128)} %bitcast.4, s32[1,1024]{1,0:T(1,128)} %bitcast.5, s32[1,256]{1,0:T(1,128)} %bitcast.6, f32[1,256]{1,0:T(1,128)} %bitcast.7), custom_call_target="tpu_custom_call" | custom-call | tf_op jit(solution)/shard_map/pallas_call | solution.py:329
  20.7 0.8 %copy.9 = f32[1024,128]{1,0:T(8,128)} copy(f32[1024,128]{1,0:T(8,128)S(1)} %shard_map.73) | data formatting | bytes 1048576

commit v6 on v5

--- a/solution.py
+++ b/solution.py
@@ -11,7 +11,7 @@
 LAG_MAX = 2
 GROUP = 8
 SPAN = 4
-PIECES = 4
+PIECES = 2
 CODE_MAX = 32767.0
 NT = (((1,), (1,)), ((), ()))
 
@@ -22,7 +22,7 @@
     out_ref,
     gain_ref, basis_ref, coef_ref, set_ref, type_ref, lag_ref, limit_ref, load_sem,
     code_send, code_pass, code_recv, unit_send, unit_pass, unit_recv, gain_far, basis_far,
-    adj_send, adj_recv, member_ref, gain_cols, basis_rows, scaled_ref, total_ref, half_recv,
+    adj_send, adj_recv, member_ref, gain_cols, basis_rows, total_ref, half_recv,
     code_ss, code_rs, unit_ss, unit_rs, pass_ss, pass_rs, adj_ss, adj_rs, half_ss, half_rs,
 ):
     my_trade = lax.axis_index("trades")
@@ -257,19 +257,15 @@
             [block[i, d] for d in range(date_count) for i in range(SPAN)], axis=0
         ).astype(jnp.bfloat16)
 
-    def scaled_of(span):
-        spread = lax.dot_general(
-            member_ref[...], block_of(span), NT, preferred_element_type=jnp.float32
-        )
-        return (spread * gain_cols[...]).astype(jnp.bfloat16)
-
-    def gradient(span, scaled):
-        rows = basis_rows[span].reshape(2 * half_rows, basis_count)
-        return jnp.dot(scaled, rows, preferred_element_type=jnp.float32)
+    def gradient(span, block, rows):
+        spread = lax.dot_general(member_ref[rows], block, NT, preferred_element_type=jnp.float32)
+        scaled = (spread * gain_cols[rows]).astype(jnp.bfloat16)
+        basis = basis_rows[span].reshape(2 * half_rows, basis_count)
+        return jnp.dot(scaled, basis, preferred_element_type=jnp.float32)
 
     def backward(step, carry):
         span = lax.rem(my_side * (spans // 2) + step, spans)
-        part = gradient(span, scaled_of(span))
+        part = gradient(span, block_of(span), pl.ds(0, trade_count))
         for q in range(2):
             columns = part[:, q * half:(q + 1) * half]
             total_ref[q] = columns if spans <= 2 else total_ref[q] + columns
@@ -288,10 +284,10 @@
     all_of(adj_recv, adj_ss.at[0], adj_rs.at[1], side).wait_recv()
     lax.fori_loop(spans // 2, spans - 1, backward, 0, unroll=spans <= 2)
     final = lax.rem(my_side * (spans // 2) + spans - 1, spans)
-    scaled_ref[...] = scaled_of(final)
+    block = block_of(final)
     for piece in range(PIECES):
         rows = pl.ds(piece * piece_rows, piece_rows)
-        part = gradient(final, scaled_ref[rows])
+        part = gradient(final, block, rows)
         for q in range(2):
             total_ref[q, rows] += part[:, q * half:(q + 1) * half]
         half_copy(piece).start()
@@ -353,7 +349,6 @@
             pltpu.VMEM((trade_count, set_count), jnp.bfloat16),
             pltpu.VMEM((trade_count, 2 * half_rows), jnp.float32),
             pltpu.VMEM((trade_peers // SPAN, 2, half_rows, basis_count), jnp.bfloat16),
-            pltpu.VMEM((trade_count, 2 * half_rows), jnp.bfloat16),
             pltpu.VMEM((2, trade_count, half), jnp.float32),
             pltpu.VMEM((trade_count, half), jnp.float32),
             dma((1,)), dma((1,)), dma((1,)), dma((1,)), dma((4,)), dma((4,)),

time: 21.8 us -> 21.8 us (level)
  no operation moved by 1% of the time
where the time goes in v6:
time: 21.8 us; the launch traced here: 21.5 us
  Pallas kernels  20.7 us (95%)
  local copies, waits for them, and re-layouts  0.8 us (4%)
    pallas_call x1, Pallas kernels, on_device(): pl.pallas_call(functools.partial(kernel, trade_peers, loss_scale), out_sh...  20.7 us
    unnamed x1, local copies, waits for them, and re-layouts  0.8 us

profile of v6, /device:TPU:1, one launch (start us, length us, event | category | flops | bytes accessed | tf_op | source)
XLA Modules:
  0.0 21.5 jit_solution(15811309797780257521)
XLA Ops:
  0.0 20.7 %shard_map.73 = f32[1024,128]{1,0:T(8,128)S(1)} custom-call(f32[4,16]{1,0:T(4,128)} %gain_in.1, bf16[4,128,256]{2,1,0:T(8,128)(2,1)} %basis_in.1, bf16[1024,256]{1,0:T(8,128)(2,1)} %coef_in.1, s32[1,1024]{1,0:T(1,128)} %bitcast.4, s32[1,1024]{1,0:T(1,128)} %bitcast.5, s32[1,256]{1,0:T(1,128)} %bitcast.6, f32[1,256]{1,0:T(1,128)} %bitcast.7), custom_call_target="tpu_custom_call" | custom-call | tf_op jit(solution)/shard_map/pallas_call | solution.py:325
  20.7 0.8 %copy.9 = f32[1024,128]{1,0:T(8,128)} copy(f32[1024,128]{1,0:T(8,128)S(1)} %shard_map.73) | data formatting | bytes 1048576

commit v7 on v6

--- a/solution.py
+++ b/solution.py
@@ -11,7 +11,6 @@
 LAG_MAX = 2
 GROUP = 8
 SPAN = 4
-PIECES = 2
 CODE_MAX = 32767.0
 NT = (((1,), (1,)), ((), ()))
 
@@ -21,7 +20,7 @@
     gain_in, basis_in, coef_in, set_in, type_in, lag_in, limit_in,
     out_ref,
     gain_ref, basis_ref, coef_ref, set_ref, type_ref, lag_ref, limit_ref, load_sem,
-    code_send, code_pass, code_recv, unit_send, unit_pass, unit_recv, gain_far, basis_far,
+    code_send, code_pass, code_recv, unit_send, unit_both, unit_recv, gain_far, basis_far,
     adj_send, adj_recv, member_ref, gain_cols, basis_rows, total_ref, half_recv,
     code_ss, code_rs, unit_ss, unit_rs, pass_ss, pass_rs, adj_ss, adj_rs, half_ss, half_rs,
 ):
@@ -137,41 +136,43 @@
     lax.fori_loop(0, 2 * core_groups, forward, 0, unroll=core_groups <= 1)
     pl.semaphore_wait(barrier, trade_peers)
     theirs = pl.ds(other_core * trade_peers, trade_peers)
-    their_paths = pl.ds(pl.multiple_of(other_core * core_paths, core_paths), core_paths)
     code_over = to_core(code_send.at[theirs], code_pass, pass_ss.at[0], pass_rs.at[0])
-    unit_over = to_core(unit_send.at[theirs], unit_pass, pass_ss.at[1], pass_rs.at[1])
+    unit_over = to_core(
+        unit_send.at[theirs], unit_both.at[my_core], pass_ss.at[1], pass_rs.at[1]
+    )
     gain_over = to_core(gain_ref, gain_far, pass_ss.at[2], pass_rs.at[2])
-    basis_over = to_core(basis_ref.at[:, their_paths], basis_far, pass_ss.at[3], pass_rs.at[3])
+    basis_over = to_core(basis_ref, basis_far, pass_ss.at[3], pass_rs.at[3])
     code_over.start()
     unit_over.start()
 
-    def deal(codes, units, first, dates):
+    def deal(codes, first, dates, units):
         def one(step, carry):
             trade = partner(trade_peers - step)
             slot = dates * trade_peers + my_trade
             to_trade(
                 codes.at[first + trade], code_recv.at[slot], code_ss.at[0], code_rs.at[0], trade
             ).start()
-            to_trade(
-                units.at[first + trade], unit_recv.at[slot], unit_ss.at[0], unit_rs.at[0], trade
-            ).start()
+            if units:
+                to_trade(
+                    unit_both.at[:, trade], unit_recv.at[my_trade], unit_ss.at[0], unit_rs.at[0], trade
+                ).start()
             return carry
 
         lax.fori_loop(1, trade_peers, one, 0, unroll=unroll)
 
+    leads = my_core == 1
     mine = my_core * trade_peers
-    deal(code_send, unit_send, mine, my_core)
+    deal(code_send, mine, my_core, False)
     code_recv[mine + my_trade] = code_send[mine + my_trade]
-    unit_recv[mine + my_trade] = unit_send[mine + my_trade]
+    unit_both[my_core] = unit_send[pl.ds(mine, trade_peers)]
     member_ref[...] = jnp.transpose(member_wide).astype(jnp.bfloat16)
     code_over.wait_recv()
     unit_over.wait_recv()
-    deal(code_pass, unit_pass, 0, other_core)
+    deal(code_pass, 0, other_core, True)
+    code_recv[other_core * trade_peers + my_trade] = code_pass[my_trade]
+    unit_recv[my_trade] = unit_both[:, my_trade]
     gain_over.start()
     basis_over.start()
-    far = other_core * trade_peers
-    code_recv[far + my_trade] = code_pass[my_trade]
-    unit_recv[far + my_trade] = unit_pass[my_trade]
 
     def widen(gains, dates):
         wide = jnp.concatenate(
@@ -180,30 +181,35 @@
         columns = pl.ds(pl.multiple_of(dates * half_rows, half_rows), half_rows)
         gain_cols[:, columns] = jnp.transpose(wide)
 
-    def order_rows(source, first, dates):
-        def one(span, carry):
-            start = pl.multiple_of(first + span * span_paths, span_paths)
+    def order_rows(source, dates):
+        def one(span, start):
             basis_rows[span, dates] = (
-                source[:, pl.ds(start, span_paths), :].reshape(half_rows, basis_count)
+                source[:, pl.ds(pl.multiple_of(start, span_paths), span_paths), :]
+                .reshape(half_rows, basis_count)
             )
+
+        def each(span, carry):
+            one(span, my_core * core_paths + span * span_paths)
             return carry
 
-        lax.fori_loop(0, spans, one, 0, unroll=spans <= 2)
-
+        lax.fori_loop(0, spans, each, 0, unroll=spans <= 2)
+        one(spans, other_core * core_paths + final * span_paths)
+
+    side = trade_peers // 2
+    my_side = my_trade // side
+    final = lax.rem(my_side * (spans // 2) + spans - 1, spans)
     widen(gains, my_core)
-    order_rows(basis_ref, my_core * core_paths, my_core)
-    if spans > 2:
-        total_ref[...] = jnp.zeros_like(total_ref)
+    order_rows(basis_ref, my_core)
 
     all_of(code_recv, code_ss.at[0], code_rs.at[0], 2 * others).wait_recv()
-    all_of(unit_recv, unit_ss.at[0], unit_rs.at[0], 2 * others).wait_recv()
+    all_of(unit_recv, unit_ss.at[0], unit_rs.at[0], others).wait_recv()
 
     def add(trade, totals):
         result = []
         for q in range(2):
             source = q * trade_peers + trade
             values = code_recv[source].astype(jnp.int32).astype(jnp.float32)
-            result.append(totals[q] + values * unit_recv[source])
+            result.append(totals[q] + values * unit_recv[trade, q])
         return tuple(result)
 
     totals = lax.fori_loop(
@@ -231,9 +237,6 @@
         parts.append(value)
     adj_send[...] = jnp.concatenate(parts, axis=0).astype(jnp.bfloat16)
 
-    side = trade_peers // 2
-    my_side = my_trade // side
-
     def adj_copy(trade):
         far = my_side + trade // side - 2 * my_side * (trade // side)
         return to_trade(adj_send, adj_recv.at[my_trade], adj_ss.at[0], adj_rs.at[far], trade)
@@ -248,62 +251,74 @@
     gain_over.wait_recv()
     basis_over.wait_recv()
     widen(gains_of(gain_far[...]), other_core)
-    order_rows(basis_far, 0, other_core)
-
-    def block_of(span):
-        block = adj_recv[pl.ds(span * SPAN, SPAN)].astype(jnp.float32)
+    order_rows(basis_far, other_core)
+
+    def scaled_of(first):
+        block = adj_recv[pl.ds(first, SPAN)].astype(jnp.float32)
         block = block.reshape(SPAN, date_count, own_paths, set_count)
-        return jnp.concatenate(
+        block = jnp.concatenate(
             [block[i, d] for d in range(date_count) for i in range(SPAN)], axis=0
         ).astype(jnp.bfloat16)
-
-    def gradient(span, block, rows):
-        spread = lax.dot_general(member_ref[rows], block, NT, preferred_element_type=jnp.float32)
-        scaled = (spread * gain_cols[rows]).astype(jnp.bfloat16)
-        basis = basis_rows[span].reshape(2 * half_rows, basis_count)
-        return jnp.dot(scaled, basis, preferred_element_type=jnp.float32)
-
-    def backward(step, carry):
+        spread = lax.dot_general(member_ref[...], block, NT, preferred_element_type=jnp.float32)
+        return (spread * gain_cols[...]).astype(jnp.bfloat16)
+
+    def backward(step, carry, fresh=False):
         span = lax.rem(my_side * (spans // 2) + step, spans)
-        part = gradient(span, block_of(span), pl.ds(0, trade_count))
+        rows = basis_rows[span].reshape(2 * half_rows, basis_count)
+        part = jnp.dot(scaled_of(span * SPAN), rows, preferred_element_type=jnp.float32)
         for q in range(2):
             columns = part[:, q * half:(q + 1) * half]
-            total_ref[q] = columns if spans <= 2 else total_ref[q] + columns
+            total_ref[q] = total_ref[q] + columns if fresh is False else columns
         return carry
 
-    piece_rows = trade_count // PIECES
-
-    def half_copy(piece):
-        rows = pl.ds(piece * piece_rows, piece_rows)
-        return to_core(
-            total_ref.at[other_core, rows], half_recv.at[rows], half_ss.at[piece], half_rs.at[piece]
-        )
-
+    def far_arrived():
+        all_of(adj_recv, adj_ss.at[0], adj_rs.at[1], side).wait_recv()
+
+    half_over = to_core(total_ref.at[other_core], half_recv, half_ss.at[0], half_rs.at[0])
+    blocks_over = to_core(
+        adj_recv.at[pl.ds(final * SPAN, SPAN)], adj_recv.at[pl.ds(trade_peers, SPAN)],
+        half_ss.at[1], half_rs.at[1],
+    )
     all_of(adj_recv, adj_ss.at[0], adj_rs.at[0], side - 1).wait_recv()
-    lax.fori_loop(0, spans // 2, backward, 0, unroll=spans <= 2)
-    all_of(adj_recv, adj_ss.at[0], adj_rs.at[1], side).wait_recv()
-    lax.fori_loop(spans // 2, spans - 1, backward, 0, unroll=spans <= 2)
-    final = lax.rem(my_side * (spans // 2) + spans - 1, spans)
-    block = block_of(final)
-    for piece in range(PIECES):
-        rows = pl.ds(piece * piece_rows, piece_rows)
-        part = gradient(final, block, rows)
-        for q in range(2):
-            total_ref[q, rows] += part[:, q * half:(q + 1) * half]
-        half_copy(piece).start()
+    backward(0, 0, True)
+    if spans > 2:
+        lax.fori_loop(1, spans // 2, backward, 0)
+
+    @pl.when(leads)
+    def _():
+        far_arrived()
+        lax.fori_loop(spans // 2, spans, backward, 0, unroll=spans <= 2)
+        half_over.start()
+        blocks_over.wait_recv()
+
+    @pl.when(jnp.logical_not(leads))
+    def _():
+        if spans > 2:
+            far_arrived()
+            lax.fori_loop(spans // 2, spans - 1, backward, 0)
+        half_over.start()
+        if spans <= 2:
+            far_arrived()
+        blocks_over.start()
+
+    half_over.wait_recv()
+    scaled = scaled_of((1 - my_core) * final * SPAN + my_core * trade_peers)
+    my_columns = pl.ds(pl.multiple_of(my_core * half, half), half)
+    rows = basis_rows[(1 - my_core) * final + my_core * spans, :, :, my_columns]
+    part = jnp.dot(
+        scaled, rows.reshape(2 * half_rows, half), preferred_element_type=jnp.float32
+    )
+    out_ref[...] = total_ref[my_core] + half_recv[...] + part
 
     all_of(code_send, code_ss.at[0], code_rs.at[0], 2 * others).wait_send()
-    all_of(unit_send, unit_ss.at[0], unit_rs.at[0], 2 * others).wait_send()
+    all_of(unit_recv, unit_ss.at[0], unit_rs.at[0], others).wait_send()
     all_of(adj_recv, adj_ss.at[0], adj_rs.at[0], others).wait_send()
-    for copy in (code_over, unit_over, gain_over, basis_over):
+    for copy in (code_over, unit_over, gain_over, basis_over, half_over):
         copy.wait_send()
-    for piece in range(PIECES):
-        rows = pl.ds(piece * piece_rows, piece_rows)
-        half_copy(piece).wait_recv()
-        out_ref[rows] = total_ref[my_core, rows] + half_recv[rows]
-
-    for piece in range(PIECES):
-        half_copy(piece).wait_send()
+
+    @pl.when(jnp.logical_not(leads))
+    def _():
+        blocks_over.wait_send()
 
 
 def on_device(
@@ -340,19 +355,19 @@
             pltpu.VMEM((trade_peers, chunk, set_count), jnp.int16),
             pltpu.VMEM((slots, chunk, set_count), jnp.int16),
             pltpu.VMEM((slots, 1, set_count), jnp.float32),
-            pltpu.VMEM((trade_peers, 1, set_count), jnp.float32),
-            pltpu.VMEM((slots, 1, set_count), jnp.float32),
+            pltpu.VMEM((2, trade_peers, 1, set_count), jnp.float32),
+            pltpu.VMEM((trade_peers, 2, 1, set_count), jnp.float32),
             pltpu.VMEM(type_gain.shape, jnp.float32),
-            pltpu.VMEM((local_dates, path_count // 2, basis_count), jnp.bfloat16),
+            pltpu.VMEM(basis_values.shape, jnp.bfloat16),
             pltpu.VMEM((2 * chunk, set_count), jnp.bfloat16),
-            pltpu.VMEM((trade_peers, 2 * chunk, set_count), jnp.bfloat16),
+            pltpu.VMEM((trade_peers + SPAN, 2 * chunk, set_count), jnp.bfloat16),
             pltpu.VMEM((trade_count, set_count), jnp.bfloat16),
             pltpu.VMEM((trade_count, 2 * half_rows), jnp.float32),
-            pltpu.VMEM((trade_peers // SPAN, 2, half_rows, basis_count), jnp.bfloat16),
+            pltpu.VMEM((trade_peers // SPAN + 1, 2, half_rows, basis_count), jnp.bfloat16),
             pltpu.VMEM((2, trade_count, half), jnp.float32),
             pltpu.VMEM((trade_count, half), jnp.float32),
             dma((1,)), dma((1,)), dma((1,)), dma((1,)), dma((4,)), dma((4,)),
-            dma((1,)), dma((2,)), dma((PIECES,)), dma((PIECES,)),
+            dma((1,)), dma((2,)), dma((2,)), dma((2,)),
         ],
         compiler_params=pltpu.CompilerParams(
             collective_id=0, has_side_effects=True, vmem_limit_bytes=vmem_limit

time: 21.8 us -> 21.5 us (0.986)
  the two profiles are of different devices: /device:TPU:1 before, /device:TPU:19 now
where the time goes in v7:
time: 21.5 us; the launch traced here: 21.3 us
  Pallas kernels  20.5 us (95%)
  local copies, waits for them, and re-layouts  0.8 us (4%)
    pallas_call x1, Pallas kernels, on_device(): pl.pallas_call(functools.partial(kernel, trade_peers, loss_scale), out_sh...  20.5 us
    unnamed x1, local copies, waits for them, and re-layouts  0.8 us

profile of v7, /device:TPU:19, one launch (start us, length us, event | category | flops | bytes accessed | tf_op | source)
XLA Modules:
  0.0 21.3 jit_solution(1685005784875035459)
XLA Ops:
  0.0 20.5 %shard_map.73 = f32[1024,128]{1,0:T(8,128)S(1)} custom-call(f32[4,16]{1,0:T(4,128)} %gain_in.1, bf16[4,128,256]{2,1,0:T(8,128)(2,1)} %basis_in.1, bf16[1024,256]{1,0:T(8,128)(2,1)} %coef_in.1, s32[1,1024]{1,0:T(1,128)} %bitcast.4, s32[1,1024]{1,0:T(1,128)} %bitcast.5, s32[1,256]{1,0:T(1,128)} %bitcast.6, f32[1,256]{1,0:T(1,128)} %bitcast.7), custom_call_target="tpu_custom_call" | custom-call | tf_op jit(solution)/shard_map/pallas_call | solution.py:340
  20.5 0.8 %copy.9 = f32[1024,128]{1,0:T(8,128)} copy(f32[1024,128]{1,0:T(8,128)S(1)} %shard_map.73) | data formatting | bytes 1048576

commit v8 on v7

--- a/solution.py
+++ b/solution.py
@@ -21,7 +21,7 @@
     out_ref,
     gain_ref, basis_ref, coef_ref, set_ref, type_ref, lag_ref, limit_ref, load_sem,
     code_send, code_pass, code_recv, unit_send, unit_both, unit_recv, gain_far, basis_far,
-    adj_send, adj_recv, member_ref, gain_cols, basis_rows, total_ref, half_recv,
+    adj_send, adj_recv, member_ref, gain_cols, basis_rows,
     code_ss, code_rs, unit_ss, unit_rs, pass_ss, pass_rs, adj_ss, adj_rs, half_ss, half_rs,
 ):
     my_trade = lax.axis_index("trades")
@@ -181,23 +181,20 @@
         columns = pl.ds(pl.multiple_of(dates * half_rows, half_rows), half_rows)
         gain_cols[:, columns] = jnp.transpose(wide)
 
+    my_columns = pl.ds(pl.multiple_of(my_core * half, half), half)
+
     def order_rows(source, dates):
-        def one(span, start):
-            basis_rows[span, dates] = (
-                source[:, pl.ds(pl.multiple_of(start, span_paths), span_paths), :]
-                .reshape(half_rows, basis_count)
-            )
-
-        def each(span, carry):
-            one(span, my_core * core_paths + span * span_paths)
+        def one(span, carry):
+            start = my_core * core_paths + span * span_paths
+            start -= (span // spans) * (2 * my_core * core_paths)
+            rows = source[:, pl.ds(pl.multiple_of(start, span_paths), span_paths), my_columns]
+            basis_rows[span, dates] = rows.reshape(half_rows, half)
             return carry
 
-        lax.fori_loop(0, spans, each, 0, unroll=spans <= 2)
-        one(spans, other_core * core_paths + final * span_paths)
+        lax.fori_loop(0, 2 * spans, one, 0, unroll=spans <= 2)
 
     side = trade_peers // 2
     my_side = my_trade // side
-    final = lax.rem(my_side * (spans // 2) + spans - 1, spans)
     widen(gains, my_core)
     order_rows(basis_ref, my_core)
 
@@ -262,63 +259,78 @@
         spread = lax.dot_general(member_ref[...], block, NT, preferred_element_type=jnp.float32)
         return (spread * gain_cols[...]).astype(jnp.bfloat16)
 
-    def backward(step, carry, fresh=False):
-        span = lax.rem(my_side * (spans // 2) + step, spans)
-        rows = basis_rows[span].reshape(2 * half_rows, basis_count)
-        part = jnp.dot(scaled_of(span * SPAN), rows, preferred_element_type=jnp.float32)
-        for q in range(2):
-            columns = part[:, q * half:(q + 1) * half]
-            total_ref[q] = total_ref[q] + columns if fresh is False else columns
-        return carry
-
-    def far_arrived():
-        all_of(adj_recv, adj_ss.at[0], adj_rs.at[1], side).wait_recv()
-
-    half_over = to_core(total_ref.at[other_core], half_recv, half_ss.at[0], half_rs.at[0])
-    blocks_over = to_core(
-        adj_recv.at[pl.ds(final * SPAN, SPAN)], adj_recv.at[pl.ds(trade_peers, SPAN)],
-        half_ss.at[1], half_rs.at[1],
-    )
-    all_of(adj_recv, adj_ss.at[0], adj_rs.at[0], side - 1).wait_recv()
-    backward(0, 0, True)
-    if spans > 2:
-        lax.fori_loop(1, spans // 2, backward, 0)
+    def backward(system, far, fresh=False):
+        which = my_side + far - 2 * my_side * far
+
+        def one(step, carry):
+            span = which * (spans // 2) + step
+            rows = basis_rows[system * spans + span].reshape(2 * half_rows, half)
+            scaled = scaled_of(system * trade_peers + span * SPAN)
+            part = jnp.dot(scaled, rows, preferred_element_type=jnp.float32)
+            out_ref[...] = part if fresh else out_ref[...] + part
+            return carry
+
+        if fresh and spans > 2:
+            out_ref[...] = jnp.zeros_like(out_ref)
+            fresh = False
+        lax.fori_loop(0, spans // 2, one, 0, unroll=spans <= 2)
+
+    def blocks_over(far):
+        first = (my_side + far - 2 * my_side * far) * side
+        return to_core(
+            adj_recv.at[pl.ds(first, side)], adj_recv.at[pl.ds(trade_peers + first, side)],
+            half_ss.at[far], half_rs.at[far],
+        )
+
+    def own_arrived(far):
+        all_of(adj_recv, adj_ss.at[0], adj_rs.at[far], side - 1 + far).wait_recv()
+        blocks_over(far).start()
 
     @pl.when(leads)
     def _():
-        far_arrived()
-        lax.fori_loop(spans // 2, spans, backward, 0, unroll=spans <= 2)
-        half_over.start()
-        blocks_over.wait_recv()
+        own_arrived(0)
 
     @pl.when(jnp.logical_not(leads))
     def _():
-        if spans > 2:
-            far_arrived()
-            lax.fori_loop(spans // 2, spans - 1, backward, 0)
-        half_over.start()
-        if spans <= 2:
-            far_arrived()
-        blocks_over.start()
-
-    half_over.wait_recv()
-    scaled = scaled_of((1 - my_core) * final * SPAN + my_core * trade_peers)
-    my_columns = pl.ds(pl.multiple_of(my_core * half, half), half)
-    rows = basis_rows[(1 - my_core) * final + my_core * spans, :, :, my_columns]
-    part = jnp.dot(
-        scaled, rows.reshape(2 * half_rows, half), preferred_element_type=jnp.float32
-    )
-    out_ref[...] = total_ref[my_core] + half_recv[...] + part
+        blocks_over(0).wait_recv()
+
+    backward(1 - my_core, 0, True)
+
+    @pl.when(leads)
+    def _():
+        own_arrived(1)
+
+    @pl.when(jnp.logical_not(leads))
+    def _():
+        own_arrived(0)
+
+    backward(0, my_core)
+
+    @pl.when(leads)
+    def _():
+        blocks_over(0).wait_recv()
+
+    @pl.when(jnp.logical_not(leads))
+    def _():
+        blocks_over(1).wait_recv()
+
+    backward(1, 1 - my_core)
+
+    @pl.when(leads)
+    def _():
+        blocks_over(1).wait_recv()
+
+    @pl.when(jnp.logical_not(leads))
+    def _():
+        own_arrived(1)
+
+    backward(my_core, 1)
 
     all_of(code_send, code_ss.at[0], code_rs.at[0], 2 * others).wait_send()
     all_of(unit_recv, unit_ss.at[0], unit_rs.at[0], others).wait_send()
     all_of(adj_recv, adj_ss.at[0], adj_rs.at[0], others).wait_send()
-    for copy in (code_over, unit_over, gain_over, basis_over, half_over):
+    for copy in (code_over, unit_over, gain_over, basis_over, blocks_over(0), blocks_over(1)):
         copy.wait_send()
-
-    @pl.when(jnp.logical_not(leads))
-    def _():
-        blocks_over.wait_send()
 
 
 def on_device(
@@ -360,12 +372,10 @@
             pltpu.VMEM(type_gain.shape, jnp.float32),
             pltpu.VMEM(basis_values.shape, jnp.bfloat16),
             pltpu.VMEM((2 * chunk, set_count), jnp.bfloat16),
-            pltpu.VMEM((trade_peers + SPAN, 2 * chunk, set_count), jnp.bfloat16),
+            pltpu.VMEM((slots, 2 * chunk, set_count), jnp.bfloat16),
             pltpu.VMEM((trade_count, set_count), jnp.bfloat16),
             pltpu.VMEM((trade_count, 2 * half_rows), jnp.float32),
-            pltpu.VMEM((trade_peers // SPAN + 1, 2, half_rows, basis_count), jnp.bfloat16),
-            pltpu.VMEM((2, trade_count, half), jnp.float32),
-            pltpu.VMEM((trade_count, half), jnp.float32),
+            pltpu.VMEM((slots // SPAN, 2, half_rows, half), jnp.bfloat16),
             dma((1,)), dma((1,)), dma((1,)), dma((1,)), dma((4,)), dma((4,)),
             dma((1,)), dma((2,)), dma((2,)), dma((2,)),
         ],

time: 21.5 us -> 21.6 us (level)
  the two profiles are of different devices: /device:TPU:19 before, /device:TPU:23 now
where the time goes in v8:
time: 21.6 us; the launch traced here: 21.4 us
  Pallas kernels  20.6 us (95%)
  local copies, waits for them, and re-layouts  0.8 us (4%)
    pallas_call x1, Pallas kernels, on_device(): pl.pallas_call(functools.partial(kernel, trade_peers, loss_scale), out_sh...  20.6 us
    unnamed x1, local copies, waits for them, and re-layouts  0.8 us

profile of v8, /device:TPU:23, one launch (start us, length us, event | category | flops | bytes accessed | tf_op | source)
XLA Modules:
  0.0 21.4 jit_solution(12957702720772491819)
XLA Ops:
  0.0 20.6 %shard_map.73 = f32[1024,128]{1,0:T(8,128)S(1)} custom-call(f32[4,16]{1,0:T(4,128)} %gain_in.1, bf16[4,128,256]{2,1,0:T(8,128)(2,1)} %basis_in.1, bf16[1024,256]{1,0:T(8,128)(2,1)} %coef_in.1, s32[1,1024]{1,0:T(1,128)} %bitcast.4, s32[1,1024]{1,0:T(1,128)} %bitcast.5, s32[1,256]{1,0:T(1,128)} %bitcast.6, f32[1,256]{1,0:T(1,128)} %bitcast.7), custom_call_target="tpu_custom_call" | custom-call | tf_op jit(solution)/shard_map/pallas_call | solution.py:352
  20.7 0.8 %copy.9 = f32[1024,128]{1,0:T(8,128)} copy(f32[1024,128]{1,0:T(8,128)S(1)} %shard_map.73) | data formatting | bytes 1048576

commit v9 on v8

--- a/solution.py
+++ b/solution.py
@@ -238,11 +238,20 @@
         far = my_side + trade // side - 2 * my_side * (trade // side)
         return to_trade(adj_send, adj_recv.at[my_trade], adj_ss.at[0], adj_rs.at[far], trade)
 
+    quarter = trade_peers // 4
+    is_last = my_trade // (3 * quarter)
+
     def spread_out(step, carry):
-        adj_copy(step + (step + trade_peers - my_trade) // trade_peers).start()
+        part = step // quarter
+        trade = step + is_last * quarter * ((part + 3) // 4 - 3 * (part // 3))
+
+        @pl.when(trade != my_trade)
+        def _():
+            adj_copy(trade).start()
+
         return carry
 
-    lax.fori_loop(0, others, spread_out, 0, unroll=unroll)
+    lax.fori_loop(0, trade_peers, spread_out, 0, unroll=unroll)
     adj_recv[my_trade] = adj_send[...]
 
     gain_over.wait_recv()

time: 21.6 us -> 21.3 us (0.986)
  the two profiles are of different devices: /device:TPU:23 before, /device:TPU:1 now
where the time goes in v9:
time: 21.3 us; the launch traced here: 21.1 us
  Pallas kernels  20.3 us (95%)
  local copies, waits for them, and re-layouts  0.8 us (4%)
    pallas_call x1, Pallas kernels, on_device(): pl.pallas_call(functools.partial(kernel, trade_peers, loss_scale), out_sh...  20.3 us
    unnamed x1, local copies, waits for them, and re-layouts  0.8 us

profile of v9, /device:TPU:1, one launch (start us, length us, event | category | flops | bytes accessed | tf_op | source)
XLA Modules:
  0.0 21.1 jit_solution(6626430707604076213)
XLA Ops:
  0.0 20.3 %shard_map.73 = f32[1024,128]{1,0:T(8,128)S(1)} custom-call(f32[4,16]{1,0:T(4,128)} %gain_in.1, bf16[4,128,256]{2,1,0:T(8,128)(2,1)} %basis_in.1, bf16[1024,256]{1,0:T(8,128)(2,1)} %coef_in.1, s32[1,1024]{1,0:T(1,128)} %bitcast.4, s32[1,1024]{1,0:T(1,128)} %bitcast.5, s32[1,256]{1,0:T(1,128)} %bitcast.6, f32[1,256]{1,0:T(1,128)} %bitcast.7), custom_call_target="tpu_custom_call" | custom-call | tf_op jit(solution)/shard_map/pallas_call | solution.py:361
  20.3 0.8 %copy.9 = f32[1024,128]{1,0:T(8,128)} copy(f32[1024,128]{1,0:T(8,128)S(1)} %shard_map.73) | data formatting | bytes 1048576

commit v10 on v9

--- a/solution.py
+++ b/solution.py
@@ -174,13 +174,6 @@
     gain_over.start()
     basis_over.start()
 
-    def widen(gains, dates):
-        wide = jnp.concatenate(
-            [jnp.broadcast_to(gains[d], (span_paths, trade_count)) for d in range(local_dates)], axis=0
-        )
-        columns = pl.ds(pl.multiple_of(dates * half_rows, half_rows), half_rows)
-        gain_cols[:, columns] = jnp.transpose(wide)
-
     my_columns = pl.ds(pl.multiple_of(my_core * half, half), half)
 
     def order_rows(source, dates):
@@ -188,14 +181,16 @@
             start = my_core * core_paths + span * span_paths
             start -= (span // spans) * (2 * my_core * core_paths)
             rows = source[:, pl.ds(pl.multiple_of(start, span_paths), span_paths), my_columns]
-            basis_rows[span, dates] = rows.reshape(half_rows, half)
+            rows = rows.astype(jnp.float32)
+            for i in range(SPAN):
+                block = rows[:, i * own_paths:(i + 1) * own_paths].reshape(chunk_rows, half)
+                basis_rows[span, i, dates] = block.astype(jnp.bfloat16)
             return carry
 
         lax.fori_loop(0, 2 * spans, one, 0, unroll=spans <= 2)
 
     side = trade_peers // 2
     my_side = my_trade // side
-    widen(gains, my_core)
     order_rows(basis_ref, my_core)
 
     all_of(code_recv, code_ss.at[0], code_rs.at[0], 2 * others).wait_recv()
@@ -256,15 +251,15 @@
 
     gain_over.wait_recv()
     basis_over.wait_recv()
-    widen(gains_of(gain_far[...]), other_core)
+    gains_far = gains_of(gain_far[...])
+    gains_all = [jnp.where(my_core == 0, near, far) for near, far in zip(gains, gains_far)]
+    gains_all += [jnp.where(my_core == 0, far, near) for near, far in zip(gains, gains_far)]
+    wide = [jnp.broadcast_to(row, (own_paths, trade_count)) for row in gains_all]
+    gain_cols[...] = jnp.transpose(jnp.concatenate(wide * SPAN, axis=0))
     order_rows(basis_far, other_core)
 
     def scaled_of(first):
-        block = adj_recv[pl.ds(first, SPAN)].astype(jnp.float32)
-        block = block.reshape(SPAN, date_count, own_paths, set_count)
-        block = jnp.concatenate(
-            [block[i, d] for d in range(date_count) for i in range(SPAN)], axis=0
-        ).astype(jnp.bfloat16)
+        block = adj_recv[pl.ds(first, SPAN)].reshape(2 * half_rows, set_count)
         spread = lax.dot_general(member_ref[...], block, NT, preferred_element_type=jnp.float32)
         return (spread * gain_cols[...]).astype(jnp.bfloat16)
 
@@ -384,7 +379,7 @@
             pltpu.VMEM((slots, 2 * chunk, set_count), jnp.bfloat16),
             pltpu.VMEM((trade_count, set_count), jnp.bfloat16),
             pltpu.VMEM((trade_count, 2 * half_rows), jnp.float32),
-            pltpu.VMEM((slots // SPAN, 2, half_rows, half), jnp.bfloat16),
+            pltpu.VMEM((slots // SPAN, SPAN, 2, chunk, half), jnp.bfloat16),
             dma((1,)), dma((1,)), dma((1,)), dma((1,)), dma((4,)), dma((4,)),
             dma((1,)), dma((2,)), dma((2,)), dma((2,)),
         ],

time: 21.3 us -> 21.3 us (level)
  no operation moved by 1% of the time
where the time goes in v10:
time: 21.3 us; the launch traced here: 21.1 us
  Pallas kernels  20.3 us (95%)
  local copies, waits for them, and re-layouts  0.8 us (4%)
    pallas_call x1, Pallas kernels, on_device(): pl.pallas_call(functools.partial(kernel, trade_peers, loss_scale), out_sh...  20.3 us
    unnamed x1, local copies, waits for them, and re-layouts  0.8 us

profile of v10, /device:TPU:1, one launch (start us, length us, event | category | flops | bytes accessed | tf_op | source)
XLA Modules:
  0.0 21.1 jit_solution(8795678100607219195)
XLA Ops:
  0.0 20.3 %shard_map.73 = f32[1024,128]{1,0:T(8,128)S(1)} custom-call(f32[4,16]{1,0:T(4,128)} %gain_in.1, bf16[4,128,256]{2,1,0:T(8,128)(2,1)} %basis_in.1, bf16[1024,256]{1,0:T(8,128)(2,1)} %coef_in.1, s32[1,1024]{1,0:T(1,128)} %bitcast.4, s32[1,1024]{1,0:T(1,128)} %bitcast.5, s32[1,256]{1,0:T(1,128)} %bitcast.6, f32[1,256]{1,0:T(1,128)} %bitcast.7), custom_call_target="tpu_custom_call" | custom-call | tf_op jit(solution)/shard_map/pallas_call | solution.py:356
  20.3 0.8 %copy.9 = f32[1024,128]{1,0:T(8,128)} copy(f32[1024,128]{1,0:T(8,128)S(1)} %shard_map.73) | data formatting | bytes 1048576

commit v11 on v10

--- a/solution.py
+++ b/solution.py
@@ -69,8 +69,10 @@
     loads = [
         pltpu.make_async_copy(source, target, load_sem.at[i])
         for i, (source, target) in enumerate((
-            (type_in, type_ref), (gain_in, gain_ref), (set_in, set_ref), (basis_in, basis_ref),
-            (coef_in, coef_ref), (lag_in, lag_ref), (limit_in, limit_ref),
+            (type_in, type_ref), (gain_in, gain_ref), (set_in, set_ref),
+            (coef_in.at[:trade_count // 2], coef_ref.at[:trade_count // 2]),
+            (coef_in.at[trade_count // 2:], coef_ref.at[trade_count // 2:]),
+            (basis_in, basis_ref), (lag_in, lag_ref), (limit_in, limit_ref),
         ))
     ]
     for load in loads:
@@ -366,7 +368,7 @@
             pltpu.VMEM((1, trade_count), jnp.int32),
             pltpu.VMEM((1, set_count), jnp.int32),
             pltpu.VMEM((1, set_count), jnp.float32),
-            dma((7,)),
+            dma((8,)),
             pltpu.VMEM((slots, chunk, set_count), jnp.int16),
             pltpu.VMEM((trade_peers, chunk, set_count), jnp.int16),
             pltpu.VMEM((slots, chunk, set_count), jnp.int16),

time: 21.3 us -> 21.3 us (level)
  no operation moved by 1% of the time
where the time goes in v11:
time: 21.3 us; the launch traced here: 21.1 us
  Pallas kernels  20.3 us (95%)
  local copies, waits for them, and re-layouts  0.8 us (4%)
    pallas_call x1, Pallas kernels, on_device(): pl.pallas_call(functools.partial(kernel, trade_peers, loss_scale), out_sh...  20.3 us
    unnamed x1, local copies, waits for them, and re-layouts  0.8 us

profile of v11, /device:TPU:1, one launch (start us, length us, event | category | flops | bytes accessed | tf_op | source)
XLA Modules:
  0.0 21.1 jit_solution(15613091296110228035)
XLA Ops:
  0.0 20.3 %shard_map.73 = f32[1024,128]{1,0:T(8,128)S(1)} custom-call(f32[4,16]{1,0:T(4,128)} %gain_in.1, bf16[4,128,256]{2,1,0:T(8,128)(2,1)} %basis_in.1, bf16[1024,256]{1,0:T(8,128)(2,1)} %coef_in.1, s32[1,1024]{1,0:T(1,128)} %bitcast.4, s32[1,1024]{1,0:T(1,128)} %bitcast.5, s32[1,256]{1,0:T(1,128)} %bitcast.6, f32[1,256]{1,0:T(1,128)} %bitcast.7), custom_call_target="tpu_custom_call" | custom-call | tf_op jit(solution)/shard_map/pallas_call | solution.py:358
  20.3 0.8 %copy.9 = f32[1024,128]{1,0:T(8,128)} copy(f32[1024,128]{1,0:T(8,128)S(1)} %shard_map.73) | data formatting | bytes 1048576

commit v12 on v11

--- a/solution.py
+++ b/solution.py
@@ -231,9 +231,11 @@
         parts.append(value)
     adj_send[...] = jnp.concatenate(parts, axis=0).astype(jnp.bfloat16)
 
+    outer = 1 - ((my_trade // (side // 2) + 1) // 2) % 2
+
     def adj_copy(trade):
         far = my_side + trade // side - 2 * my_side * (trade // side)
-        return to_trade(adj_send, adj_recv.at[my_trade], adj_ss.at[0], adj_rs.at[far], trade)
+        return to_trade(adj_send, adj_recv.at[my_trade], adj_ss.at[0], adj_rs.at[far * (1 + outer)], trade)
 
     quarter = trade_peers // 4
     is_last = my_trade // (3 * quarter)
@@ -281,16 +283,19 @@
             fresh = False
         lax.fori_loop(0, spans // 2, one, 0, unroll=spans <= 2)
 
-    def blocks_over(far):
-        first = (my_side + far - 2 * my_side * far) * side
+    def blocks_over(level):
+        first = (my_side * side, (2 - my_side) * (side // 2), (3 - 3 * my_side) * (side // 2))[level]
+        count = side if level == 0 else side // 2
         return to_core(
-            adj_recv.at[pl.ds(first, side)], adj_recv.at[pl.ds(trade_peers + first, side)],
-            half_ss.at[far], half_rs.at[far],
+            adj_recv.at[pl.ds(first, count)], adj_recv.at[pl.ds(trade_peers + first, count)],
+            half_ss.at[level], half_rs.at[level],
         )
 
     def own_arrived(far):
-        all_of(adj_recv, adj_ss.at[0], adj_rs.at[far], side - 1 + far).wait_recv()
-        blocks_over(far).start()
+        for level in (1, 2) if far else (0,):
+            count = side // 2 if far else side - 1
+            all_of(adj_recv, adj_ss.at[0], adj_rs.at[level], count).wait_recv()
+            blocks_over(level).start()
 
     @pl.when(leads)
     def _():
@@ -319,12 +324,14 @@
     @pl.when(jnp.logical_not(leads))
     def _():
         blocks_over(1).wait_recv()
+        blocks_over(2).wait_recv()
 
     backward(1, 1 - my_core)
 
     @pl.when(leads)
     def _():
         blocks_over(1).wait_recv()
+        blocks_over(2).wait_recv()
 
     @pl.when(jnp.logical_not(leads))
     def _():
@@ -335,7 +342,7 @@
     all_of(code_send, code_ss.at[0], code_rs.at[0], 2 * others).wait_send()
     all_of(unit_recv, unit_ss.at[0], unit_rs.at[0], others).wait_send()
     all_of(adj_recv, adj_ss.at[0], adj_rs.at[0], others).wait_send()
-    for copy in (code_over, unit_over, gain_over, basis_over, blocks_over(0), blocks_over(1)):
+    for copy in (code_over, unit_over, gain_over, basis_over, *map(blocks_over, range(3))):
         copy.wait_send()
 
 
@@ -383,7 +390,7 @@
             pltpu.VMEM((trade_count, 2 * half_rows), jnp.float32),
             pltpu.VMEM((slots // SPAN, SPAN, 2, chunk, half), jnp.bfloat16),
             dma((1,)), dma((1,)), dma((1,)), dma((1,)), dma((4,)), dma((4,)),
-            dma((1,)), dma((2,)), dma((2,)), dma((2,)),
+            dma((1,)), dma((3,)), dma((3,)), dma((3,)),
         ],
         compiler_params=pltpu.CompilerParams(
             collective_id=0, has_side_effects=True, vmem_limit_bytes=vmem_limit

time: 21.3 us -> 21.3 us (level)
  no operation moved by 1% of the time
where the time goes in v12:
time: 21.3 us; the launch traced here: 21.1 us
  Pallas kernels  20.3 us (95%)
  local copies, waits for them, and re-layouts  0.8 us (4%)
    pallas_call x1, Pallas kernels, on_device(): pl.pallas_call(functools.partial(kernel, trade_peers, loss_scale), out_sh...  20.3 us
    unnamed x1, local copies, waits for them, and re-layouts  0.8 us

profile of v12, /device:TPU:1, one launch (start us, length us, event | category | flops | bytes accessed | tf_op | source)
XLA Modules:
  0.0 21.1 jit_solution(16219415870113033452)
XLA Ops:
  0.0 20.3 %shard_map.73 = f32[1024,128]{1,0:T(8,128)S(1)} custom-call(f32[4,16]{1,0:T(4,128)} %gain_in.1, bf16[4,128,256]{2,1,0:T(8,128)(2,1)} %basis_in.1, bf16[1024,256]{1,0:T(8,128)(2,1)} %coef_in.1, s32[1,1024]{1,0:T(1,128)} %bitcast.4, s32[1,1024]{1,0:T(1,128)} %bitcast.5, s32[1,256]{1,0:T(1,128)} %bitcast.6, f32[1,256]{1,0:T(1,128)} %bitcast.7), custom_call_target="tpu_custom_call" | custom-call | tf_op jit(solution)/shard_map/pallas_call | solution.py:365
  20.3 0.8 %copy.9 = f32[1024,128]{1,0:T(8,128)} copy(f32[1024,128]{1,0:T(8,128)S(1)} %shard_map.73) | data formatting | bytes 1048576
